TPU v7x, 256 devices: a whole 4x4x8 slice. The times are simulated.
256 devices in a mesh: seq: 32 (over x, z), head: 8 (over y, core).
Axes of the slice: x: 4, y: 4, z: 8, core: 2. Of those that a mesh axis runs over, the one named last changes fastest.
Arguments:
- tokens: bfloat16 [16384, 2048], P('seq', 'head'), may hold values from -6 to 6
- weight_x: bfloat16 [2048, 4096], P(None, 'head'), may hold values from -0.125 to 0.125
- weight_z: bfloat16 [2048, 4096], P(None, 'head'), may hold values from -0.125 to 0.125
- weight_bc: bfloat16 [2048, 256], replicated, may hold values from -0.125 to 0.125
- weight_dt: bfloat16 [64, 2048], P('head'), may hold values from -0.125 to 0.125
- conv_x_weight: float32 [4, 4096], P(None, 'head'), may hold values from -3 to 3
- conv_x_bias: float32 [4096], P('head'), may hold values from -3 to 3
- conv_bc_weight: float32 [4, 256], replicated, may hold values from -3 to 3
- conv_bc_bias: float32 [256], replicated, may hold values from -3 to 3
- step_bias: float32 [64], P('head'), may hold values from -4.5 to -2.5
- decay_log: float32 [64], P('head')
- skip_gain: float32 [64], P('head'), may hold values from 0.5 to 1.5
- norm_gain: float32 [4096], P('head'), may hold values from 0.1 to 1.9
- lengths: int32 [8], replicated, may hold values from 1 to 8192, 16384 in all
- page_table: int32 [8], replicated, may hold values from 0 to 31, as said below
Outputs:
- normed: bfloat16 [16384, 4096], P('seq', 'head')
- ssm_pages: float32 [32, 64, 64, 128], P('seq', 'head')
- conv_x_pages: float32 [32, 3, 4096], P('seq', None, 'head')
- conv_bc_pages: float32 [32, 3, 256], P('seq')
Inputs may be any that keep to these rules, and one draw needn't show every extreme that they name: The lengths sum to 16384, and the longest is exactly 8192. `page_table`: the pages of different prompts differ; the last prompt's page is 30.
All inputs are finite; a program needn't handle non-finite values.
Results may differ from a plain program's by a relative error of at most 0.015.
Values may be sent and summed in bfloat16 or wider, within the bound.
A program may use at most 64 MiB of HBM per device.

v0:
```python
import jax
import jax.numpy as jnp
from jax import lax
from jax.sharding import PartitionSpec as P

GROUP = 256


norm_epsilon = 1e-05


def from_behind(x, axis, by):
    size = lax.axis_size(axis)
    pairs = [(i, i + by) for i in range(size) if 0 <= i + by < size]
    return lax.ppermute(x, axis, pairs)


def prefix(value, axis, join, neutral):
    count, mine = (lax.axis_size(axis), lax.axis_index(axis))
    pieces = jax.tree.map(lambda part: lax.all_gather(part, axis), value)
    total = jax.tree.map(
        lambda part, zero: jnp.full_like(part, 0) + jnp.asarray(zero, part.dtype), value, neutral
    )

    def step(position, total):
        longer = join(total, jax.tree.map(lambda part: part[position], pieces))
        return jax.tree.map(lambda new, old: jnp.where(position < mine, new, old), longer, total)

    return lax.fori_loop(0, count - 1, step, total)


def segment_of(starts, positions):
    return jnp.sum((starts[None, :] <= positions[:, None]).astype(jnp.int32), axis=1) - 1


def causal_conv(extended, conv_weight, conv_bias, segments_ext, count):
    tap_count = conv_weight.shape[0]
    own_segment = segments_ext[tap_count - 1 : tap_count - 1 + count]
    running = jnp.zeros((count, extended.shape[1]), jnp.float32) + conv_bias[None, :]
    for tap_index in range(tap_count):
        same_prompt = (segments_ext[tap_index : tap_index + count] == own_segment)[:, None]
        running = running + jnp.where(
            same_prompt,
            extended[tap_index : tap_index + count].astype(jnp.float32)
            * conv_weight[tap_index][None, :],
            0.0,
        )
    return jax.nn.silu(running).astype(jnp.bfloat16)


def group_local(x_group, b_group, c_group, dt_group, la_group, seg_group, reset_group):
    length = x_group.shape[0]
    cumulative = jnp.cumsum(la_group, axis=1)
    position_index = jnp.arange(length)
    keep_mask = (position_index[:, None] >= position_index[None, :]) & (
        seg_group[:, None] == seg_group[None, :]
    )
    gaps = jnp.where(keep_mask[None], cumulative[:, :, None] - cumulative[:, None, :], 0.0)
    decay_mask = jnp.where(keep_mask[None], jnp.exp(gaps), 0.0)
    scores = jnp.dot(c_group, b_group.T, preferred_element_type=jnp.float32)
    weights = (scores[None] * decay_mask).astype(jnp.bfloat16)
    x_values = x_group.astype(jnp.float32)
    x_scaled = (dt_group.T[:, :, None] * x_values).astype(jnp.bfloat16)
    within = jnp.einsum("hij,jhp->ihp", weights, x_scaled, preferred_element_type=jnp.float32)
    keep_last = seg_group == seg_group[length - 1]
    to_last = jnp.where(
        keep_last[None],
        jnp.exp(jnp.where(keep_last[None], cumulative[:, length - 1 :] - cumulative, 0.0)),
        0.0,
    )
    x_weighted = ((to_last * dt_group).T[:, :, None] * x_values).astype(jnp.bfloat16)
    state_now = jnp.einsum("jhp,jn->hpn", x_weighted, b_group, preferred_element_type=jnp.float32)
    unbroken = jnp.cumsum(reset_group.astype(jnp.int32)) == 0
    decay_rate = jnp.where(unbroken[length - 1], jnp.exp(cumulative[:, length - 1]), 0.0)
    inflow = jnp.where(unbroken[None, :], jnp.exp(cumulative), 0.0)
    return (within, state_now, decay_rate, inflow)


def final_state(x_group, b_group, dt_group, la_group, seg_group, reset_group, spot_index, entering):
    length = x_group.shape[0]
    cumulative = jnp.cumsum(la_group, axis=1)
    position_index = jnp.arange(length)
    keep_mask = (position_index <= spot_index) & (seg_group == seg_group[spot_index])
    cum_spot = cumulative[:, spot_index]
    to_spot = jnp.where(
        keep_mask[None],
        jnp.exp(jnp.where(keep_mask[None], cum_spot[:, None] - cumulative, 0.0)),
        0.0,
    )
    x_weighted = ((to_spot * dt_group).T[:, :, None] * x_group.astype(jnp.float32)).astype(
        jnp.bfloat16
    )
    from_group = jnp.einsum("jhp,jn->hpn", x_weighted, b_group, preferred_element_type=jnp.float32)
    unbroken = jnp.cumsum(reset_group.astype(jnp.int32))[spot_index] == 0
    inflow_spot = jnp.where(unbroken, jnp.exp(cum_spot), 0.0)
    return from_group + inflow_spot[:, None, None] * entering


def body(
    tokens,
    weight_x,
    weight_z,
    weight_bc,
    weight_dt,
    conv_x_weight,
    conv_x_bias,
    conv_bc_weight,
    conv_bc_bias,
    step_bias,
    decay_log,
    skip_gain,
    norm_gain,
    lengths,
    page_table,
):
    tok_rows = tokens.shape[0]
    inner_dev = weight_x.shape[1]
    heads_dev = weight_dt.shape[0]
    head_width = inner_dev // heads_dev
    width_bc = weight_bc.shape[1]
    state_width = width_bc // 2
    tap_count = conv_x_weight.shape[0]
    prompt_count = lengths.shape[0]
    seq_index = lax.axis_index("seq")
    block_start = seq_index * tok_rows

    def project(shard_piece, matrix):
        return jnp.dot(shard_piece, matrix, preferred_element_type=jnp.float32)

    shard_piece = lax.all_gather(tokens, "head", axis=1, tiled=True)
    acc_x = project(shard_piece, weight_x)
    acc_z = project(shard_piece, weight_z)
    dt_raw = lax.dot_general(
        weight_dt, shard_piece, (((1,), (1,)), ((), ())), preferred_element_type=jnp.float32
    )
    acc_bc = project(shard_piece, weight_bc)
    bc_in = acc_bc.astype(jnp.bfloat16)
    x_in = acc_x.astype(jnp.bfloat16)
    z_in = acc_z.astype(jnp.bfloat16)
    starts = jnp.cumsum(lengths) - lengths
    prompt_ends = starts + lengths - 1
    positions = block_start + jnp.arange(tok_rows, dtype=jnp.int32)
    segments = segment_of(starts, positions)
    resets = jnp.any(starts[None, :] == positions[:, None], axis=1)
    ext_positions = (
        block_start - (tap_count - 1) + jnp.arange(tok_rows + tap_count - 1, dtype=jnp.int32)
    )
    segments_ext = segment_of(starts, ext_positions)
    joined = jnp.concatenate([x_in, bc_in], axis=1)
    previous_tail = from_behind(joined[tok_rows - (tap_count - 1) :], "seq", 1)
    extended = jnp.concatenate([previous_tail, joined], axis=0)
    conv_weight = jnp.concatenate([conv_x_weight, conv_bc_weight], axis=1)
    conv_bias = jnp.concatenate([conv_x_bias, conv_bc_bias], axis=0)
    conv_out = causal_conv(extended, conv_weight, conv_bias, segments_ext, tok_rows)
    x_conv = conv_out[:, :inner_dev]
    b_conv = conv_out[:, inner_dev : inner_dev + state_width]
    c_conv = conv_out[:, inner_dev + state_width :]
    step_size = jax.nn.softplus(dt_raw + step_bias[:, None])
    log_decay = -step_size * jnp.exp(decay_log)[:, None]
    group_count = tok_rows // GROUP
    x_all = x_conv.reshape(group_count, GROUP, heads_dev, head_width)
    b_all = b_conv.reshape(group_count, GROUP, state_width)
    c_all = c_conv.reshape(group_count, GROUP, state_width)
    dt_all = step_size.reshape(heads_dev, group_count, GROUP).transpose(1, 0, 2)
    la_all = log_decay.reshape(heads_dev, group_count, GROUP).transpose(1, 0, 2)
    seg_all = segments.reshape(group_count, GROUP)
    reset_all = resets.reshape(group_count, GROUP)

    def local_group(inputs):
        return group_local(*inputs)

    within_all, state_all, decay_all, inflow_all = lax.map(
        local_group, (x_all, b_all, c_all, dt_all, la_all, seg_all, reset_all)
    )

    def link_step(carried, inputs):
        held_state, product = carried
        decay_rate, state_now = inputs
        return (
            (decay_rate[:, None, None] * held_state + state_now, decay_rate * product),
            (held_state, product),
        )

    empty_state = jnp.zeros((heads_dev, head_width, state_width), jnp.float32)
    unit_decay = jnp.ones((heads_dev,), jnp.float32)
    (block_state, block_decay), (held_local, decay_before) = lax.scan(
        link_step, (empty_state, unit_decay), (decay_all, state_all)
    )

    def combine(earlier, later):
        return (earlier[0] * later[0], later[0][:, None, None] * earlier[1] + later[1])

    _, incoming = prefix((block_decay, block_state), "seq", combine, (unit_decay, empty_state))
    entering_all = held_local + decay_before[:, :, None, None] * incoming[None]
    across = (
        jnp.einsum(
            "cin,chpn->cihp",
            c_all,
            entering_all.astype(jnp.bfloat16),
            preferred_element_type=jnp.float32,
        )
        * inflow_all.transpose(0, 2, 1)[:, :, :, None]
    )
    ssd_out = (
        within_all + across + skip_gain[None, None, :, None] * x_all.astype(jnp.float32)
    ).astype(jnp.bfloat16)
    ssd_flat = ssd_out.reshape(tok_rows, inner_dev)
    gated_out = ssd_flat.astype(jnp.float32) * jax.nn.silu(z_in.astype(jnp.float32))
    square_total = lax.psum(jnp.sum(gated_out * gated_out, axis=1), "head")
    inner_total = inner_dev * lax.axis_size("head")
    normed = (
        gated_out
        * lax.rsqrt(square_total / inner_total + norm_epsilon)[:, None]
        * norm_gain[None, :]
    ).astype(jnp.bfloat16)
    ends_here = prompt_ends // tok_rows == seq_index
    local_end = jnp.clip(prompt_ends - block_start, 0, tok_rows - 1)
    group_pick = local_end // GROUP
    spots = local_end % GROUP
    finals = jax.vmap(final_state)(
        x_all[group_pick],
        b_all[group_pick],
        dt_all[group_pick],
        la_all[group_pick],
        seg_all[group_pick],
        reset_all[group_pick],
        spots,
        entering_all[group_pick],
    )
    finals = jnp.where(ends_here[:, None, None, None], finals, 0.0)

    def conv_rows(end_local, owner):
        picked = lax.dynamic_slice_in_dim(extended, end_local + 1, tap_count - 1, 0)
        picked_seg = lax.dynamic_slice_in_dim(segments_ext, end_local + 1, tap_count - 1, 0)
        return jnp.where((picked_seg == owner)[:, None], picked.astype(jnp.float32), 0.0)

    kept_rows = jax.vmap(conv_rows)(local_end, jnp.arange(prompt_count, dtype=jnp.int32))
    kept_rows = jnp.where(ends_here[:, None, None], kept_rows, 0.0)
    kept_x = kept_rows[:, :, :inner_dev]
    kept_bc = kept_rows[:, :, inner_dev:]
    page_hits = (
        page_table[:, None] == jnp.arange(lax.axis_size("seq"), dtype=jnp.int32)[None, :]
    ).astype(jnp.float32)
    pool_ssm = jnp.einsum("rq,rhpn->qhpn", page_hits, finals, precision=lax.Precision.HIGHEST)
    pool_x = jnp.einsum("rq,rkc->qkc", page_hits, kept_x, precision=lax.Precision.HIGHEST)
    pool_bc = jnp.einsum("rq,rkc->qkc", page_hits, kept_bc, precision=lax.Precision.HIGHEST)
    ssm_page, conv_x_page, conv_bc_page = (
        lax.psum_scatter(
            pool_ssm.astype(jnp.bfloat16), "seq", scatter_dimension=0, tiled=True
        ).astype(jnp.float32),
        lax.psum_scatter(
            pool_x.astype(jnp.bfloat16), "seq", scatter_dimension=0, tiled=True
        ).astype(jnp.float32),
        lax.psum_scatter(
            pool_bc.astype(jnp.bfloat16), "seq", scatter_dimension=0, tiled=True
        ).astype(jnp.float32),
    )
    return (normed, ssm_page, conv_x_page, conv_bc_page)


def solution(mesh):
    in_specs = (
        P("seq", "head"),
        P(None, "head"),
        P(None, "head"),
        P(),
        P("head", None),
        P(None, "head"),
        P("head"),
        P(),
        P(),
        P("head"),
        P("head"),
        P("head"),
        P("head"),
        P(),
        P(),
    )
    out_specs = (
        P("seq", "head"),
        P("seq", "head", None, None),
        P("seq", None, "head"),
        P("seq", None, None),
    )
    return jax.shard_map(body, mesh=mesh, in_specs=in_specs, out_specs=out_specs, check_vma=False)
```

profile of v0, /device:TPU:1, one launch (start us, length us, event | category | flops | bytes accessed | tf_op | source)
XLA Modules:
  0.0 599.1 jit_solution(13054633298480660735)
XLA Ops:
  13.3 30.6 %all-gather.5.cloned.1.call-done = bf16[512,2048]{1,0:T(8,128)(2,1)} async-done(((bf16[512,256]{1,0:T(8,128)(2,1)}), bf16[512,2048]{1,0:T(8,128)(2,1)}) %all-gather.5.cloned.1.call-update) | async-done | bytes 2097168 | tf_op jit(solution)/shard_map/all_gather | solution.py:130
  43.9 2.8 convolution_convert_fusion.3
  46.7 2.9 convolution_convert_fusion.2
  49.8 3.2 collective-permute-start
  53.0 1.3 negate_multiply_fusion
  54.3 2.7 collective-permute-done
  57.5 2.2 multiply_convert_fusion.6
  63.9 45.2 %while.48 = (s32[]{:T(128)}, f32[2,256,8,64]{1,3,2,0:T(8,128)}, f32[2,8,64,128]{3,2,1,0:T(8,128)S(1)}, f32[2,8]{1,0:T(2,128)}, f32[2,8,256]{2,1,0:T(8,128)}, /*i...) while((s32[]{:T(128)}, f32[2,256,8,64]{1,3,2,0:T(8,128)}, ...), condition=%wide.region_9.10_spmd, body=%wide.region_4.9_spmd.sunk | while | flops 121352992 | bytes 2354508 | solution.py:172
  64.5 1.8 compare_reduce_fusion.3
  68.0 1.3 reduce-window.59
  70.7 1.3 dynamic-slice_bitcast_fusion.6
  74.0 1.3 reduce-window.57
  76.6 1.3 select_reduce_fusion.2
  79.2 1.4 fusion.103
  84.2 2.3 fusion.100
  87.1 1.8 compare_reduce_fusion.3
  93.3 1.3 dynamic-slice_bitcast_fusion.6
  96.6 1.3 reduce-window.57
  99.2 1.3 select_reduce_fusion.2
  101.8 1.4 fusion.103
  106.8 2.4 fusion.100
  110.5 7.9 %while.50 = (s32[]{:T(128)}, f32[8,64,128]{2,1,0:T(8,128)S(1)}, f32[8]{0:T(128)}, f32[2,8,64,128]{3,2,1,0:T(8,128)}, f32[2,8]{1,0:T(2,128)}, /*index=5*/f32[2,8]...) while((s32[]{:T(128)}, f32[8,64,128]{2,1,0:T(8,128)S(1)}, f32[8]{0:T(128)}, ...), condition=%wide.region_11.12_spmd.clone, body=%wide.region_10.11_spmd.clone.sunk | while | flops 262163 | bytes 1311105 | solution.py:186
  128.9 4.5 reduce-window.38
  133.8 1.3 copy.97
  137.2 2.2 copy.102
  140.1 2.0 gather_fusion.3
  142.0 16.2 %while.49 = (s32[]{:T(128)}, bf16[515,768]{1,0:T(8,128)(2,1)}, s32[8,2]{0,1:T(2,128)S(1)}, bf16[8,3,768]{2,1,0:T(4,128)(2,1)S(1)}, s32[]{:T(128)}) while((s32[]{:T(128)}, bf16[515,768]{1,0:T(8,128)(2,1)}, s32[8,2]{0,1:T(2,128)S(1)}, bf16[8,3,768]{2,1,0:T(4,128)(2,1)S(1)}, s32[]{:T(128)}) %tuple.144), condition=%wide.while_cond, body=%wide.while_body.sunk | while | flops 2 | bytes 10857 | solution.py:233
  142.7 1.4 bitcast_dynamic-update-slice_fusion.4
  144.7 1.4 bitcast_dynamic-update-slice_fusion.4
  146.7 1.4 bitcast_dynamic-update-slice_fusion.4
  148.8 1.4 bitcast_dynamic-update-slice_fusion.4
  150.8 1.4 bitcast_dynamic-update-slice_fusion.4
  152.8 1.4 bitcast_dynamic-update-slice_fusion.4
  154.9 1.4 bitcast_dynamic-update-slice_fusion.4
  156.9 1.4 bitcast_dynamic-update-slice_fusion.4
  160.3 63.6 %all-reduce.2 = f32[256]{0:T(256)S(1)} all-reduce(f32[256]{0:T(256)S(1)} %dynamic-update-slice.2), channel_id=2, replica_groups=mesh['seq'=32,'head'=8] {'seq'}, use_global_device_ids=true, to_apply=%add.2 | all-reduce | flops 256 | bytes 2048
  224.2 34.0 %while.51 = (s32[]{:T(128)}, f32[8,64,128]{2,1,0:T(8,128)S(1)}, s32[]{:T(128)}, f32[32,8]{1,0:T(8,128)S(1)}, f32[32,8,64,128]{3,2,1,0:T(8,128)}, /*index=5*/s32[]{:T(128)}, s32[]{:T(128)}) while((s32[]{:T(128)}, f32[8,64,128]{2,1,0:T(8,128)S(1)}, s32[]{:T(128)}, f32[32,8]{1,0:T(8,128)S(1)}, f32[32,8,64,128]{3,2,1,0:T(8,128)}, ...), condition=%wide.region_13.14_spmd.clone, body=%wide.region_12.13_spmd.clone.sunk | while | flops 262148 | bytes 786641 | solution.py:29
  259.5 2.0 gather_fusion.6
  261.5 3.0 add_select_fusion
  264.5 4.0 convolution_convert_fusion
  268.5 3.5 copy.101
  273.2 110.4 %all-reduce.4 = bf16[32,3,256]{2,1,0:T(4,128)(2,1)S(1)} all-reduce(bf16[32,3,256]{2,1,0:T(4,128)(2,1)S(1)} %copy.105), channel_id=6, replica_groups=mesh['seq'=32,'head'=8] {'seq'}, use_global_device_ids=true, to_apply=%region_22.23.clone | all-reduce | flops 24576 | bytes 98304
  386.6 1.5 fusion.41
  389.8 2.5 multiply_reduce_fusion
  392.3 53.8 %psum.7 = f32[512]{0:T(512)S(1)} all-reduce(f32[512]{0:T(512)S(1)} %get-tuple-element.449), channel_id=1, replica_groups=mesh['seq'=32,'head'=8] {'head'}, use_global_device_ids=true, to_apply=%region_15.16 | all-reduce | flops 512 | bytes 4096 | tf_op jit(solution)/shard_map/psum | solution.py:209
  446.1 1.4 multiply_convert_fusion.7
  448.5 142.4 %reduce-scatter.2.cloned.1.call-done = bf16[1,8,64,128]{3,2,1,0:T(8,128)(2,1)} async-done(((bf16[32,8,64,128]{3,2,1,0:T(8,128)(2,1)}), bf16[1,8,64,128]{3,2,1,0:T(8,128)(2,1)}) %reduce-scatter.2.cloned.1.call-update) | async-done | bytes 131088 | tf_op jit(solution)/shard_map/reduce_scatter | solution.py:248
  590.9 1.6 convert_element_type.136
  (299 shorter events, 106.3 us)
Async XLA Ops:
  7.2 381.9 %copy-start = (bf16[2048,512]{1,0:T(8,128)(2,1)S(1)}, bf16[2048,512]{1,0:T(8,128)(2,1)}, u32[]{:S(2)}) copy-start(bf16[2048,512]{1,0:T(8,128)(2,1)} %param.23) | copy-start | bytes 6291460
  7.2 36.7 %all-gather.5.cloned.1.call-start = ((), (), s32[]{:S(2)}) async-start(), calls=%async_computation.1 | async-start | bytes 2359296 | tf_op jit(solution)/shard_map/all_gather | solution.py:130
  7.9 216.3 %all-gather.7.cloned.1.call-start = ((), (), s32[]{:S(2)}) async-start(), calls=%async_computation.3 | async-start | bytes 8650752 | tf_op jit(solution)/shard_map/all_gather | solution.py:20
  8.8 1.9 copy-start.28
  43.9 2.8 copy-start.5
  46.7 6.3 %copy-start.19 = (bf16[8,2048]{1,0:T(8,128)(2,1)S(1)}, bf16[8,2048]{1,0:T(8,128)(2,1)}, u32[]{:S(2)}) copy-start(bf16[8,2048]{1,0:T(8,128)(2,1)} %param.25) | copy-start | bytes 98308
  46.7 6.3 %copy-start.33 = (f32[8]{0:T(128)S(1)}, f32[8]{0:T(128)}, u32[]{:S(2)}) copy-start(f32[8]{0:T(128)} %param.30) | copy-start | bytes 100
  49.8 7.2 %collective-permute-start = (bf16[3,768]{0,1:T(8,128)(2,1)S(1)}, bf16[3,768]{0,1:T(8,128)(2,1)S(1)}, u32[]{:S(2)}, u32[]{:S(2)}) collective-permute-start(bf16[3,768]{0,1:T(8,128)(2,1)S(1)} %fusion.48), channel_id=1, source_target_pairs={{0,8},{8,16},{16,24},{24,32},{32,40},{40,48},{48,56},{56,64},{64,7... | collective-permute-start | bytes 13832 | tf_op jit(solution)/shard_map/ppermute | solution.py:15
  57.5 2.9 copy-start.2
  60.6 2.8 copy-start.3
  61.8 0.7 copy-start.9
  63.9 6.8 %copy-start.12 = (pred[2,256]{1,0:T(4,128)(4,1)}, pred[2,256]{1,0:T(4,128)(4,1)S(1)}, u32[]{:S(2)}) copy-start(pred[2,256]{1,0:T(4,128)(4,1)S(1)} %get-tuple-element.686) | copy-start | bytes 1540 | tf_op jit(solution)/shard_map/while
  70.1 0.6 copy-start.17
  75.9 2.0 copy-start.16
  76.0 0.6 copy-start.8
  84.2 2.4 copy-start.13
  86.5 6.8 %copy-start.12 = (pred[2,256]{1,0:T(4,128)(4,1)}, pred[2,256]{1,0:T(4,128)(4,1)S(1)}, u32[]{:S(2)}) copy-start(pred[2,256]{1,0:T(4,128)(4,1)S(1)} %get-tuple-element.686) | copy-start | bytes 1540 | tf_op jit(solution)/shard_map/while
  92.7 0.6 copy-start.17
  98.5 2.0 copy-start.16
  98.6 0.6 copy-start.8
  106.7 2.4 copy-start.13
  118.5 0.7 copy-start.1
  118.5 6.8 %copy-start.31 = (u32[256]{0:T(256)S(1)}, u32[256]{0:T(256)}, u32[]{:S(2)}) copy-start(u32[256]{0:T(256)} %constant.239) | copy-start | bytes 3076
  118.5 8.6 %copy-start.29 = (s32[8,1]{0,1:T(1,128)S(1)}, s32[8,1]{0,1:T(1,128)}, u32[]{:S(2)}) copy-start(s32[8,1]{0,1:T(1,128)} %copy-done.28) | copy-start | bytes 100
  118.5 9.1 %copy-start.30 = (s32[8]{0:T(128)S(1)}, s32[8]{0:T(128)}, u32[]{:S(2)}) copy-start(s32[8]{0:T(128)} %get-tuple-element.444) | copy-start | bytes 100
  118.5 9.2 %copy-start.7 = (f32[2,8,256]{2,1,0:T(8,128)S(1)}, f32[2,8,256]{2,1,0:T(8,128)}, u32[]{:S(2)}) copy-start(f32[2,8,256]{2,1,0:T(8,128)} %get-tuple-element.766) | copy-start | bytes 49156
  118.5 9.8 %copy-start.11 = (f32[2,8,256]{2,1,0:T(8,128)S(1)}, f32[2,8,256]{2,1,0:T(8,128)}, u32[]{:S(2)}) copy-start(f32[2,8,256]{2,1,0:T(8,128)} %get-tuple-element.767) | copy-start | bytes 49156
  119.2 265.5 %all-reduce.7.cloned.1.call-start = ((), (), s32[]{:S(2)}) async-start(), calls=%async_computation.4 | async-start | bytes 262144
  140.0 2.0 copy-start.18
  140.0 18.3 %copy-start.25 = (pred[8]{0:T(512)(128)(4,1)S(1)}, pred[8]{0:T(512)(128)(4,1)}, u32[]{:S(2)}) copy-start(pred[8]{0:T(512)(128)(4,1)} %fusion.66) | copy-start | bytes 28
  140.0 18.3 %copy-start.27 = (pred[8,3]{0,1:T(4,128)(4,1)S(1)}, pred[8,3]{0,1:T(4,128)(4,1)}, u32[]{:S(2)}) copy-start(pred[8,3]{0,1:T(4,128)(4,1)} %add_compare_fusion) | copy-start | bytes 76
  140.0 19.0 %copy-start.22 = (s32[8]{0:T(128)S(1)}, s32[8]{0:T(128)}, u32[]{:S(2)}) copy-start(s32[8]{0:T(128)} %param.35) | copy-start | bytes 100
  140.0 20.0 %copy-start.21 = (f32[8]{0:T(128)S(1)}, f32[8]{0:T(128)}, u32[]{:S(2)}) copy-start(f32[8]{0:T(128)} %get-tuple-element.208) | copy-start | bytes 100
  158.4 0.6 copy-start.14
  223.9 34.3 %copy-start.32 = (f32[2,8]{1,0:T(2,128)S(1)}, f32[2,8]{1,0:T(2,128)}, u32[]{:S(2)}) copy-start(f32[2,8]{1,0:T(2,128)} %get-tuple-element.207) | copy-start | bytes 196
  223.9 367.0 %reduce-scatter.2.cloned.1.call-start = ((), (), s32[]{:S(2)}) async-start(), calls=%async_computation.2 | async-start | bytes 4325376 | tf_op jit(solution)/shard_map/reduce_scatter | solution.py:248
  259.4 2.1 copy-start.15
  259.4 2.0 copy-start.26
  261.5 3.0 copy-start.23
  272.0 114.6 %copy-start.4 = (bf16[2,256,8,64]{1,0,3,2:T(2,128)(2,1)S(1)}, bf16[2,256,8,64]{1,0,3,2:T(2,128)(2,1)}, u32[]{:S(2)}) copy-start(bf16[2,256,8,64]{1,0,3,2:T(2,128)(2,1)} %copy-done.3) | copy-start | bytes 1572868
  272.0 114.6 %copy-start.10 = (bf16[2,256,128]{1,0,2:T(2,128)(2,1)S(1)}, bf16[2,256,128]{1,0,2:T(2,128)(2,1)}, u32[]{:S(2)}) copy-start(bf16[2,256,128]{1,0,2:T(2,128)(2,1)} %copy-done.9) | copy-start | bytes 393220
  272.0 114.6 %copy-start.20 = (f32[2,8,256]{2,1,0:T(8,128)S(1)}, f32[2,8,256]{2,1,0:T(8,128)}, u32[]{:S(2)}) copy-start(f32[2,8,256]{2,1,0:T(8,128)} %get-tuple-element.211) | copy-start | bytes 49156
  272.0 114.6 %copy-start.34 = (f32[8]{0:T(128)S(1)}, f32[8]{0:T(128)}, u32[]{:S(2)}) copy-start(f32[8]{0:T(128)} %param.32) | copy-start | bytes 100
  388.2 1.6 copy-start.6
  389.8 56.3 %copy-start.24 = (f32[512]{0:T(512)S(1)}, f32[512]{0:T(512)}, u32[]{:S(2)}) copy-start(f32[512]{0:T(512)} %param.33) | copy-start | bytes 6148
Sparse Core Ops, SparseCore 0:
  9.8 34.0 all-gather.4
  119.3 102.3 all-gather.6
  225.2 143.1 all-reduce.6
  372.7 218.1 reduce-scatter.1
where the time goes:
time: 606 us; the launch traced here: 599 us
  blocking collectives  228 us (38%)
  waiting for transfers between devices  177 us (29%)
  other arithmetic  80.3 us (13%)
  local copies, waits for them, and re-layouts  68 us (11%)
  matrix products  26.6 us (4%)
  between operations  15.1 us (2%)
    unnamed x2, blocking collectives  174 us
    reduce_scatter x1, waiting for transfers between devices, body(): lax.psum_scatter(pool_ssm.astype(jnp.bfloat16), 'seq', scatter_dimension=...  142 us
    psum x1, blocking collectives, body(): square_total = lax.psum(jnp.sum(gated_out * gated_out, axis=1), 'head')  53.8 us
    select_n x31, other arithmetic, step(): jnp.where(position < mine, new, old)  32.7 us
    all_gather x1, waiting for transfers between devices, body(): shard_piece = lax.all_gather(tokens, 'head', axis=1, tiled=True)  30.6 us
    gather x24, local copies, waits for them, and re-layouts  16.1 us
    another operation x17, other arithmetic  15.9 us
  transfers between devices with their start and end apart: 5, of which 3 were waited for; matrix products, arithmetic and copies ran while one was open for 17% of the time, Pallas kernels for 0%

commit v1 on v0

v1 whole, which is shorter than its diff:
```python
import functools

import jax
import jax.numpy as jnp
from jax import lax
from jax.experimental import pallas as pl
from jax.experimental.pallas import tpu as pltpu
from jax.sharding import PartitionSpec as P

MESH = pl.DeviceIdType.MESH
F32 = jnp.float32
BF16 = jnp.bfloat16
EPS = 1e-05
HALO = 16
LOG2E = 1.4426950408889634


def vmem():
    return pl.BlockSpec(memory_space=pltpu.VMEM)


def hbm():
    return pl.BlockSpec(memory_space=pl.ANY)


def smem():
    return pl.BlockSpec(memory_space=pltpu.SMEM)


def project_kernel(
    nseq, nhead,
    tok, wx, wz, wbc, wdt,
    u_out, z_out, dt_out,
    tokbuf, w, wdtp, acc, accdt,
    lsem, ssem, rsem, hs_sem, hr_sem,
):
    ny = nhead // 2
    seq = lax.axis_index("seq")
    head = lax.axis_index("head")
    y = head // 2
    core = head % 2
    rows, feat = tok.shape
    half = rows // 2
    inner = wx.shape[1]
    wide = wbc.shape[1]
    heads = wdt.shape[0]
    yp, ym = (y + 1) % ny, (y + ny - 1) % ny
    y2 = (y + 2) % ny
    up, down = yp * 2 + core, ym * 2 + core
    other = y * 2 + (1 - core)
    nxt, prv = (seq + 1) % nseq, (seq + nseq - 1) % nseq
    lanes = pl.ds(pl.multiple_of(core * feat, feat), feat)
    other_lanes = pl.ds(pl.multiple_of((1 - core) * feat, feat), feat)
    first, second = pl.ds(HALO, half), pl.ds(HALO + half, half)
    both = pl.ds(HALO, rows)
    edge = pl.ds(0, HALO)

    loads = [
        pltpu.make_async_copy(tok, tokbuf.at[y, both, lanes], lsem.at[0]),
        pltpu.make_async_copy(wx, w.at[:, pl.ds(0, inner)], lsem.at[1]),
        pltpu.make_async_copy(wbc, w.at[:, pl.ds(2 * inner, wide)], lsem.at[2]),
        pltpu.make_async_copy(wz, w.at[:, pl.ds(inner, inner)], lsem.at[3]),
        pltpu.make_async_copy(wdt, wdtp.at[pl.ds(0, heads)], lsem.at[4]),
    ]

    barrier = pltpu.get_barrier_semaphore()
    for k in range(1, nhead):
        pl.semaphore_signal(
            barrier, inc=1, device_id={"head": (head + k) % nhead}, device_id_type=MESH
        )
    pl.semaphore_signal(barrier, inc=1, device_id={"seq": nxt}, device_id_type=MESH)
    pl.semaphore_signal(barrier, inc=1, device_id={"seq": prv}, device_id_type=MESH)
    wdtp[pl.ds(heads, 128 - heads), :] = jnp.zeros((128 - heads, wdtp.shape[1]), BF16)
    for one in loads:
        one.start()
    pl.semaphore_wait(barrier, nhead + 1)

    sent = []

    def send(src, dst, number, to):
        copy = pltpu.make_async_remote_copy(
            src_ref=src, dst_ref=dst, send_sem=ssem.at[number], recv_sem=rsem.at[number],
            device_id=to, device_id_type=MESH,
        )
        copy.start()
        sent.append(copy)

    def arrive(region, number):
        pltpu.make_async_remote_copy(
            src_ref=region, dst_ref=region, send_sem=ssem.at[number], recv_sem=rsem.at[number],
            device_id={"head": other}, device_id_type=MESH,
        ).wait_recv()

    to_up, to_down, to_other = {"head": up}, {"head": down}, {"head": other}
    mine = tokbuf.at[y]
    send(tok.at[pl.ds(rows - HALO, HALO)], mine.at[edge, lanes], 13, {"seq": nxt})
    send(tok.at[pl.ds(0, half)], mine.at[first, lanes], 1, to_up)
    send(tok.at[pl.ds(half, half)], mine.at[second, lanes], 3, to_down)
    send(tok, mine.at[both, lanes], 0, to_other)
    send(tok.at[pl.ds(half, half)], mine.at[second, lanes], 2, to_up)
    send(tok.at[pl.ds(0, half)], mine.at[first, lanes], 4, to_down)

    def halo_piece(owner):
        return tokbuf.at[
            owner // 2, edge, pl.ds(pl.multiple_of((owner % 2) * feat, feat), feat)
        ]

    arrive(halo_piece(head), 13)
    halo_sends = []
    for k in range(1, nhead):
        copy = pltpu.make_async_remote_copy(
            src_ref=halo_piece(head), dst_ref=halo_piece(head),
            send_sem=hs_sem.at[k], recv_sem=hr_sem.at[head],
            device_id={"head": (head + k) % nhead}, device_id_type=MESH,
        )
        copy.start()
        halo_sends.append(copy)

    def halo_arrive(owner):
        pltpu.make_async_remote_copy(
            src_ref=halo_piece(owner), dst_ref=halo_piece(owner),
            send_sem=hs_sem.at[0], recv_sem=hr_sem.at[owner],
            device_id={"head": other}, device_id_type=MESH,
        ).wait_recv()

    tile = 256
    tiles = (2 * inner + wide) // tile

    def multiply(at, start):
        k = pl.ds(pl.multiple_of(at * 2 * feat, 2 * feat), 2 * feat)

        @pl.loop(0, tiles)
        def _(n):
            cols = pl.ds(pl.multiple_of(n * tile, tile), tile)
            part = jnp.dot(tokbuf[at], w[k, cols], preferred_element_type=F32)
            if start:
                acc[:, cols] = part
            else:
                acc[:, cols] += part

        part = lax.dot_general(
            tokbuf[at, both, :], wdtp[:, k], (((1,), (1,)), ((), ())),
            preferred_element_type=F32,
        )
        if start:
            accdt[...] = part
        else:
            accdt[...] += part

    for one in loads:
        one.wait()
    arrive(mine.at[both, other_lanes], 0)
    halo_arrive(other)
    multiply(y, True)

    arrive(tokbuf.at[ym, first, lanes], 1)
    send(tokbuf.at[ym, first, lanes], tokbuf.at[ym, first, lanes], 5, to_up)
    arrive(tokbuf.at[yp, second, lanes], 3)
    send(tokbuf.at[yp, second, lanes], tokbuf.at[yp, second, lanes], 6, to_down)
    send(tokbuf.at[ym, first, lanes], tokbuf.at[ym, first, lanes], 7, to_other)
    send(tokbuf.at[yp, second, lanes], tokbuf.at[yp, second, lanes], 9, to_other)
    arrive(tokbuf.at[ym, second, lanes], 2)
    send(tokbuf.at[ym, second, lanes], tokbuf.at[ym, second, lanes], 8, to_other)
    arrive(tokbuf.at[yp, first, lanes], 4)
    send(tokbuf.at[yp, first, lanes], tokbuf.at[yp, first, lanes], 10, to_other)
    arrive(tokbuf.at[ym, first, other_lanes], 7)
    arrive(tokbuf.at[ym, second, other_lanes], 8)
    halo_arrive(ym * 2)
    halo_arrive(ym * 2 + 1)
    multiply(ym, False)
    arrive(tokbuf.at[yp, second, other_lanes], 9)
    arrive(tokbuf.at[yp, first, other_lanes], 10)
    halo_arrive(yp * 2)
    halo_arrive(yp * 2 + 1)
    multiply(yp, False)

    arrive(tokbuf.at[y2, first, lanes], 5)
    send(tokbuf.at[y2, first, lanes], tokbuf.at[y2, first, lanes], 11, to_other)
    arrive(tokbuf.at[y2, second, lanes], 6)
    send(tokbuf.at[y2, second, lanes], tokbuf.at[y2, second, lanes], 12, to_other)
    halo_arrive(y2 * 2)
    halo_arrive(y2 * 2 + 1)
    arrive(tokbuf.at[y2, first, other_lanes], 11)
    arrive(tokbuf.at[y2, second, other_lanes], 12)
    multiply(y2, False)

    u_out[:, pl.ds(0, inner)] = acc[:, pl.ds(0, inner)].astype(BF16)
    u_out[:, pl.ds(inner, wide)] = acc[:, pl.ds(2 * inner, wide)].astype(BF16)
    z_out[...] = acc[pl.ds(HALO, rows), pl.ds(inner, inner)].astype(BF16)
    dt_out[...] = accdt[...]
    for copy in sent + halo_sends:
        copy.wait_send()


def project(tokens, weight_x, weight_z, weight_bc, weight_dt, nseq, nhead, interpret=False):
    rows, feat = tokens.shape
    depth, inner = weight_x.shape
    wide = weight_bc.shape[1]
    total = 2 * inner + wide
    return pl.pallas_call(
        functools.partial(project_kernel, nseq, nhead),
        name="project",
        out_shape=(
            jax.ShapeDtypeStruct((rows + HALO, inner + wide), BF16),
            jax.ShapeDtypeStruct((rows, inner), BF16),
            jax.ShapeDtypeStruct((rows, 128), F32),
        ),
        in_specs=[hbm()] * 5,
        out_specs=(vmem(), vmem(), vmem()),
        scratch_shapes=[
            pltpu.VMEM((nhead // 2, rows + HALO, 2 * feat), BF16),
            pltpu.VMEM((depth, total), BF16),
            pltpu.VMEM((128, depth), BF16),
            pltpu.VMEM((rows + HALO, total), F32),
            pltpu.VMEM((rows, 128), F32),
            pltpu.SemaphoreType.DMA((5,)),
            pltpu.SemaphoreType.DMA((14,)),
            pltpu.SemaphoreType.DMA((14,)),
            pltpu.SemaphoreType.DMA((nhead,)),
            pltpu.SemaphoreType.DMA((nhead,)),
        ],
        compiler_params=pltpu.CompilerParams(
            collective_id=0, has_side_effects=True, vmem_limit_bytes=48 << 20
        ),
    )(tokens, weight_x, weight_z, weight_bc, weight_dt)


def read_prompts(len_ref, count):
    starts, ends = [], []
    at = jnp.int32(0)
    for r in range(count):
        starts.append(at)
        at = at + len_ref[r]
        ends.append(at - 1)
    return starts, ends


def ends_in_block(starts, ends, base, rows):
    count = len(starts)
    none = jnp.int32(-1)
    a_start, a_end = none, none
    b_start, b_end = none, none
    a_at = none
    for r in range(count - 1, -1, -1):
        here = (ends[r] >= base) & (ends[r] < base + rows)
        a_start = jnp.where(here, starts[r], a_start)
        a_end = jnp.where(here, ends[r], a_end)
        a_at = jnp.where(here, r, a_at)
    for r in range(count):
        here = (ends[r] >= base) & (ends[r] < base + rows) & (a_at != r)
        b_start = jnp.where(here, starts[r], b_start)
        b_end = jnp.where(here, ends[r], b_end)
    return a_start, a_end, b_start, b_end


def end_slots(starts, ends, rows):
    prompts = len(starts)
    slot, block = [], []
    for r in range(prompts):
        at = ends[r] // rows
        a = jnp.bool_(True) if r == 0 else (ends[r - 1] // rows) != at
        b = jnp.bool_(True) if r == prompts - 1 else (ends[r + 1] // rows) != at
        slot.append(jnp.where(a, 0, jnp.where(b, 1, 2)).astype(jnp.int32))
        block.append(at)
    return slot, block


def local_kernel(
    len_ref, page_ref, u, dt_raw, wconv_x, bconv_x, wconv_bc, bconv_bc, step_bias, decay_log,
    skip,
    s_out, d_out, ab_out, v_out, y_out, c_out, col_out, more_out,
    uf, xc, bcol, ccol, btr, scores, stage,
):
    rows = y_out.shape[0]
    inner = y_out.shape[1]
    state = c_out.shape[1]
    heads = step_bias.shape[0]
    lbs = inner // 128
    prompts = len_ref.shape[0]
    base = lax.axis_index("seq") * rows
    starts, ends = read_prompts(len_ref, prompts)

    def start_of(pos):
        found = jnp.zeros_like(pos)
        for r in range(prompts):
            found = jnp.where(starts[r] <= pos, starts[r], found)
        return found

    pos_col = base + lax.broadcasted_iota(jnp.int32, (rows, 1), 0)
    start_col = start_of(pos_col)
    stage[...] = jnp.broadcast_to((pos_col - start_col).astype(F32), stage.shape)
    width = u.shape[1]
    taps = wconv_x.shape[0]
    step = 32

    @pl.loop(0, rows // step)
    def _(t):
        r0 = pl.multiple_of(t * step, step)
        age = stage[pl.ds(r0, step), :]
        for j in range(width // 128):
            lanes = pl.ds(j * 128, 128)
            win = u[pl.ds(r0, step + HALO), lanes].astype(F32)
            uf[pl.ds(r0, step + HALO), lanes] = win
            if j < lbs:
                wl, wt, wb = lanes, wconv_x, bconv_x
            else:
                wl, wt, wb = pl.ds((j - lbs) * 128, 128), wconv_bc, bconv_bc
            total = jnp.broadcast_to(wb[:, wl], (step, 128))
            for k in range(taps):
                d = taps - 1 - k
                shifted = win if d == 0 else pltpu.roll(win, d, 0)
                term = shifted[HALO:, :] * wt[pl.ds(k, 1), wl]
                total = total + (term if d == 0 else jnp.where(age >= d, term, 0.0))
            out = jax.nn.silu(total)
            if j < lbs:
                xc[pl.ds(r0, step), lanes] = out.astype(BF16)
            elif j == lbs:
                bcol[pl.ds(r0, step), :] = out.astype(BF16).astype(F32)
            else:
                ccol[pl.ds(r0, step), :] = out.astype(BF16)

    c_out[...] = ccol[...]
    btr[...] = jnp.transpose(bcol[...]).astype(BF16)

    dtr = jnp.transpose(dt_raw[...])[0:heads, :]
    pre = dtr + step_bias[...]
    dt = jnp.maximum(pre, 0.0) + jnp.log1p(jnp.exp(-jnp.abs(pre)))
    cum = -dt * jnp.exp(decay_log[...])
    lane = lax.broadcasted_iota(jnp.int32, (heads, rows), 1)
    shift = 1
    while shift < rows:
        cum = cum + jnp.where(lane >= shift, pltpu.roll(cum, shift, 1), 0.0)
        shift *= 2
    pos = base + lane
    start_row = start_of(pos)
    a_start, a_end, b_start, b_end = ends_in_block(starts, ends, base, rows)
    more = jnp.int32(0)
    for kind in end_slots(starts, ends, rows)[0]:
        more = jnp.maximum(more, kind - 1)
    more_out[0] = more
    last_start = start_of(jnp.full((heads, rows), base + rows - 1, jnp.int32))

    def at_pos(where_pos):
        return jnp.sum(jnp.where(pos == where_pos, cum, 0.0), axis=1, keepdims=True)

    cum_last = at_pos(base + rows - 1)
    cum_a, cum_b = at_pos(a_end), at_pos(b_end)

    def weight_to(cum_end, keep):
        return jnp.where(keep, jnp.exp(jnp.minimum(cum_end - cum, 0.0)), 0.0) * dt

    w_end = weight_to(cum_last, pos >= last_start)
    w_a = weight_to(cum_a, (pos >= a_start) & (pos <= a_end))
    w_b = weight_to(cum_b, (pos >= b_start) & (pos <= b_end))
    inflow = jnp.where(start_row < base, jnp.exp(cum), 0.0)
    decay = jnp.where(last_start[:, 0:1] < base, jnp.exp(cum_last), 0.0)
    decay_a = jnp.where(
        (jnp.full((heads, 1), a_start) < base) & (jnp.full((heads, 1), a_end) >= 0),
        jnp.exp(cum_a), 0.0,
    )
    cum2 = cum * LOG2E
    packed = jnp.concatenate(
        [cum2, inflow, w_end, w_a, w_b]
        + [jnp.zeros((128 - 5 * heads, rows), F32)], axis=0,
    )
    cols = jnp.transpose(packed)
    col_out[...] = cols
    low = lax.broadcasted_iota(jnp.int32, (rows, 128), 1) < 64
    low_row = lax.broadcasted_iota(jnp.int32, (1, 128), 1) < 64

    for lb in range(lbs):
        h0, h1 = 2 * lb, 2 * lb + 1
        for k, value in enumerate((decay, decay_a)):
            d_out[lb, pl.ds(k, 1), :] = jnp.where(
                low_row,
                jnp.broadcast_to(value[h0 : h0 + 1, :], (1, 128)),
                jnp.broadcast_to(value[h1 : h1 + 1, :], (1, 128)),
            )

    per = s_out.shape[0] // lbs
    piece = state // per
    for lb in range(lbs):
        x_lb = xc[:, pl.ds(lb * 128, 128)].astype(F32)
        for kind in range(3):
            at = (2 + kind) * heads + 2 * lb
            scale = jnp.where(low, cols[:, at : at + 1], cols[:, at + 1 : at + 2])
            weighted = (x_lb * scale).astype(BF16)
            value = jnp.dot(btr[...], weighted, preferred_element_type=F32).astype(BF16)
            value = value.reshape(per, piece, 128)
            if kind == 0:
                s_out[pl.ds(lb * per, per)] = value
            else:
                ab_out[pl.ds(lb * per, per), kind - 1] = value

    tile = 128
    blocks = rows // tile
    for i in range(blocks):
        ri = pl.ds(i * tile, tile)
        reach = (i + 1) * tile
        sc = jnp.dot(ccol[ri, :], btr[:, 0:reach], preferred_element_type=F32)
        pi = base + i * tile + lax.broadcasted_iota(jnp.int32, (tile, reach), 0)
        pj = base + lax.broadcasted_iota(jnp.int32, (tile, reach), 1)
        si = start_col[i * tile : reach, :]
        sc = jnp.where((pj <= pi) & (pj >= si), sc, 0.0)
        scores[ri, 0:reach] = sc
    low_t = lax.broadcasted_iota(jnp.int32, (tile, 128), 1) < 64
    for lb in range(lbs):
        lanes = pl.ds(lb * 128, 128)
        for i in range(blocks):
            ri = pl.ds(i * tile, tile)
            reach = (i + 1) * tile
            parts = []
            for hh in range(2):
                h = 2 * lb + hh
                gap = jnp.minimum(
                    cols[i * tile : reach, h : h + 1] - cum2[h : h + 1, 0:reach], 0.0
                )
                wgt = (scores[ri, 0:reach] * jnp.exp2(gap) * dt[h : h + 1, 0:reach]).astype(BF16)
                parts.append(jnp.dot(wgt, xc[0:reach, lanes], preferred_element_type=F32))
            y_out[ri, lanes] = (
                jnp.where(low_t, parts[0], parts[1])
                + skip[:, lanes] * xc[ri, lanes].astype(F32)
            )

    v_out[...] = jnp.zeros(v_out.shape, BF16)
    zero_rows = jnp.zeros((32, 128), F32)
    for r in range(prompts):
        @pl.when((ends[r] >= base) & (ends[r] < base + rows))
        def _():
            stage[pl.ds(0, 32), :] = zero_rows
            local = ends[r] - base + HALO
            for k in range(taps - 1):
                back = taps - 2 - k
                line = uf[pl.ds(local - back, 1), :]
                keep = jnp.full((1, 128), ends[r] - back, jnp.int32) >= starts[r]
                for j in range(lbs):
                    stage[k * lbs + j : k * lbs + j + 1, :] = jnp.where(
                        keep, line[:, j * 128 : (j + 1) * 128], 0.0
                    )
                for j in range(2):
                    at = (taps - 1) * lbs + 2 * k + j
                    stage[at : at + 1, :] = jnp.where(
                        keep, line[:, (lbs + j) * 128 : (lbs + j + 1) * 128], 0.0
                    )
            v_out[page_ref[r]] = stage[pl.ds(0, 32), :].astype(BF16)


def local(u, dt_raw, wconv_x, bconv_x, wconv_bc, bconv_bc, step_bias, decay_log, skip,
          lengths, pages, nseq):
    rows = dt_raw.shape[0]
    inner = wconv_x.shape[1]
    state = wconv_bc.shape[1] // 2
    lbs = inner // 128
    piece = state * lbs // nseq
    return pl.pallas_call(
        local_kernel,
        name="local",
        out_shape=(
            jax.ShapeDtypeStruct((nseq, piece, 128), BF16),
            jax.ShapeDtypeStruct((lbs, 2, 128), F32),
            jax.ShapeDtypeStruct((nseq, 2, piece, 128), BF16),
            jax.ShapeDtypeStruct((nseq, 32, 128), BF16),
            jax.ShapeDtypeStruct((rows, inner), F32),
            jax.ShapeDtypeStruct((rows, state), BF16),
            jax.ShapeDtypeStruct((rows, 128), F32),
            jax.ShapeDtypeStruct((1,), jnp.int32),
        ),
        in_specs=[smem(), smem()] + [vmem()] * 9,
        out_specs=(vmem(),) * 7 + (smem(),),
        scratch_shapes=[
            pltpu.VMEM((rows + HALO, u.shape[1]), F32),
            pltpu.VMEM((rows, inner), BF16),
            pltpu.VMEM((rows, state), F32),
            pltpu.VMEM((rows, state), BF16),
            pltpu.VMEM((state, rows), BF16),
            pltpu.VMEM((rows, rows), F32),
            pltpu.VMEM((rows, 128), F32),
        ],
        compiler_params=pltpu.CompilerParams(vmem_limit_bytes=48 << 20),
    )(lengths, pages, u, dt_raw, wconv_x, bconv_x, wconv_bc, bconv_bc, step_bias, decay_log, skip)


def finish_kernel(
    nseq, nhead, heads,
    len_ref, page_ref, s_in, d_in, ab_in, v_in, y_in, c_in, col_in, z_in, gain,
    n_out, page_out, cx_out, cb_out,
    s_buf, d_buf, ab_buf, v_buf, h_all, h_send, h_buf, p_send, p_buf, q_send, q_buf, gated,
    send_sem, recv_sem, qs_sem, qr_sem,
):
    seq = lax.axis_index("seq")
    head = lax.axis_index("head")
    rows, inner = y_in.shape
    lbs = inner // 128
    per = nseq // lbs
    piece = s_in.shape[1]
    state = per * piece
    prompts = len_ref.shape[0]
    lb_me = seq // per

    barrier = pltpu.get_barrier_semaphore()

    @pl.loop(1, nseq)
    def _(d):
        pl.semaphore_signal(
            barrier, inc=1, device_id={"seq": (seq + d) % nseq}, device_id_type=MESH
        )

    for k in range(1, nhead):
        pl.semaphore_signal(
            barrier, inc=1, device_id={"head": (head + k) % nhead}, device_id_type=MESH
        )
    s_buf[seq] = s_in[seq]
    d_buf[seq] = d_in[lb_me]
    ab_buf[seq] = ab_in[seq]
    v_buf[seq] = v_in[seq]
    pl.semaphore_wait(barrier, nseq - 1 + nhead - 1)

    S, D, AB, V, H, PG = range(6)

    def copy(kind, src, dst, d, to):
        return pltpu.make_async_remote_copy(
            src_ref=src, dst_ref=dst, send_sem=send_sem.at[kind, d], recv_sem=recv_sem.at[kind, d],
            device_id={"seq": to}, device_id_type=MESH,
        )

    def out_copy(kind, d):
        to = (seq + d) % nseq
        if kind == S:
            return copy(S, s_in.at[to], s_buf.at[seq], d, to)
        if kind == D:
            return copy(D, d_in.at[to // per], d_buf.at[seq], d, to)
        if kind == AB:
            return copy(AB, ab_in.at[to], ab_buf.at[seq], d, to)
        if kind == V:
            return copy(V, v_in.at[to], v_buf.at[seq], d, to)
        if kind == H:
            return copy(H, h_send.at[to], h_buf.at[seq], d, to)
        return copy(PG, p_send.at[to], p_buf.at[seq], d, to)

    def in_copy(kind, d):
        frm = (seq + nseq - d) % nseq
        buf = (s_buf, d_buf, ab_buf, v_buf, h_buf, p_buf)[kind]
        return copy(kind, buf.at[frm], buf.at[frm], d, frm)

    def start_all(*kinds):
        @pl.loop(1, nseq)
        def _(d):
            for kind in kinds:
                out_copy(kind, d).start()

    def arrive_all(*kinds):
        @pl.loop(1, nseq)
        def _(d):
            for kind in kinds:
                in_copy(kind, d).wait_recv()

    start_all(S, D)
    start_all(AB)
    arrive_all(S, D)

    def advance(i, carried):
        h_all[i] = carried
        h_send[i] = carried.astype(BF16)
        return d_buf[i, 0:1, :] * carried + s_buf[i].astype(F32)

    lax.fori_loop(0, nseq, advance, jnp.zeros((piece, 128), F32))
    start_all(H)
    h_buf[seq] = h_send[seq]
    start_all(V)

    starts, ends = read_prompts(len_ref, prompts)
    slot, block = end_slots(starts, ends, rows)
    arrive_all(AB)

    @pl.loop(0, nseq)
    def _(q):
        kind = jnp.int32(2)
        at = jnp.int32(0)
        for r in range(prompts):
            hit = page_ref[r] == q
            kind = jnp.where(hit, slot[r], kind)
            at = jnp.where(hit, block[r], at)
        which = jnp.where(kind == 1, 1, 0)
        at = jnp.clip(at, 0, nseq - 1)
        value = ab_buf[at, which].astype(F32)
        first = value + d_buf[at, 1:2, :] * h_all[at]
        kinds = jnp.full((piece, 128), kind, jnp.int32)
        p_send[q] = jnp.where(kinds == 0, first, jnp.where(kinds == 1, value, 0.0)).astype(BF16)

    start_all(PG)
    p_buf[seq] = p_send[seq]

    arrive_all(H)
    tile = 64
    low = lax.broadcasted_iota(jnp.int32, (tile, 128), 1) < 64
    lanes128 = lax.broadcasted_iota(jnp.int32, (tile, 128), 1)
    subl = lax.broadcasted_iota(jnp.int32, (tile, 128), 0)
    per_row = 128 // tile

    for g in range(rows // 128):
        line = jnp.zeros((1, 128), F32)
        for s in range(per_row):
            r0 = g * 128 + s * tile
            ri = pl.ds(r0, tile)
            total = jnp.zeros((tile, 128), F32)
            for lb in range(lbs):
                lanes = pl.ds(lb * 128, 128)
                hmat = h_buf[pl.ds(lb * per, per)].reshape(state, 128)
                ac = jnp.dot(c_in[ri, :], hmat, preferred_element_type=F32)
                at = heads + 2 * lb
                scale = jnp.where(low, col_in[ri, at : at + 1], col_in[ri, at + 1 : at + 2])
                yv = (y_in[ri, lanes] + ac * scale).astype(BF16).astype(F32)
                zv = z_in[ri, lanes].astype(F32)
                gv = yv * jax.nn.silu(zv)
                gated[ri, lanes] = gv
                total = total + gv * gv
            col = jnp.sum(total, axis=1, keepdims=True)
            line = line + jnp.sum(
                jnp.where(lanes128 == subl + s * tile, col, 0.0), axis=0, keepdims=True
            )
        q_send[g : g + 1, :] = line

    q_copies = []
    for k in range(1, nhead):
        one = pltpu.make_async_remote_copy(
            src_ref=q_send, dst_ref=q_buf.at[head], send_sem=qs_sem.at[k], recv_sem=qr_sem.at[k],
            device_id={"head": (head + k) % nhead}, device_id_type=MESH,
        )
        one.start()
        q_copies.append(one)
    q_buf[head] = q_send[...]

    arrive_all(V)
    source = jnp.int32(0)
    found = jnp.int32(0)
    for r in range(prompts):
        hit = page_ref[r] == seq
        source = jnp.where(hit, block[r], source)
        found = jnp.where(hit, 1, found)
    source = jnp.clip(source, 0, nseq - 1)
    vv = jnp.where(
        jnp.full(v_buf.shape[1:], found, jnp.int32) == 1, v_buf[source].astype(F32), 0.0
    )
    kept = cx_out.shape[0]
    for k in range(kept):
        for j in range(lbs):
            cx_out[k : k + 1, j * 128 : (j + 1) * 128] = vv[k * lbs + j : k * lbs + j + 1, :]
        for j in range(2):
            at = kept * lbs + 2 * k + j
            cb_out[k : k + 1, j * 128 : (j + 1) * 128] = vv[at : at + 1, :]

    for k in range(1, nhead):
        frm = (head + nhead - k) % nhead
        pltpu.make_async_remote_copy(
            src_ref=q_send, dst_ref=q_buf.at[frm], send_sem=qs_sem.at[k], recv_sem=qr_sem.at[k],
            device_id={"head": frm}, device_id_type=MESH,
        ).wait_recv()
    squares = q_buf[0]
    for k in range(1, nhead):
        squares = squares + q_buf[k]
    scale_rows = lax.rsqrt(squares / (inner * nhead) + EPS)
    for g in range(rows // 128):
        for s in range(per_row):
            ri = pl.ds(g * 128 + s * tile, tile)
            diag = jnp.where(lanes128 == subl + s * tile, scale_rows[g : g + 1, :], 0.0)
            scale = jnp.sum(diag, axis=1, keepdims=True)
            n_out[ri, :] = (gated[ri, :] * scale * gain[...]).astype(BF16)

    arrive_all(PG)
    for lb in range(lbs):
        mat = p_buf[pl.ds(lb * per, per)].reshape(state, 128).astype(F32)
        page_out[pl.ds(lb * 128, 128), :] = jnp.transpose(mat)

    @pl.loop(1, nseq)
    def _(d):
        for kind in (S, D, AB, V, H, PG):
            out_copy(kind, d).wait_send()

    for one in q_copies:
        one.wait_send()


def finish(s, d, ab, v, y, c, col, z, gain, lengths, pages, heads, kept, nseq, nhead):
    rows, inner = y.shape
    state = c.shape[1]
    piece = s.shape[1]
    wide = 2 * state
    return pl.pallas_call(
        functools.partial(finish_kernel, nseq, nhead, heads),
        name="finish",
        out_shape=(
            jax.ShapeDtypeStruct((rows, inner), BF16),
            jax.ShapeDtypeStruct((inner, state), F32),
            jax.ShapeDtypeStruct((kept, inner), F32),
            jax.ShapeDtypeStruct((kept, wide), F32),
        ),
        in_specs=[smem(), smem()] + [vmem()] * 9,
        out_specs=(vmem(),) * 4,
        scratch_shapes=[
            pltpu.VMEM(s.shape, BF16),
            pltpu.VMEM((nseq, 2, 128), F32),
            pltpu.VMEM(ab.shape, BF16),
            pltpu.VMEM(v.shape, BF16),
            pltpu.VMEM((nseq, piece, 128), F32),
            pltpu.VMEM((nseq, piece, 128), BF16),
            pltpu.VMEM((nseq, piece, 128), BF16),
            pltpu.VMEM((nseq, piece, 128), BF16),
            pltpu.VMEM((nseq, piece, 128), BF16),
            pltpu.VMEM((rows // 128, 128), F32),
            pltpu.VMEM((nhead, rows // 128, 128), F32),
            pltpu.VMEM((rows, inner), F32),
            pltpu.SemaphoreType.DMA((6, nseq)),
            pltpu.SemaphoreType.DMA((6, nseq)),
            pltpu.SemaphoreType.DMA((nhead,)),
            pltpu.SemaphoreType.DMA((nhead,)),
        ],
        compiler_params=pltpu.CompilerParams(
            collective_id=1, has_side_effects=True, vmem_limit_bytes=48 << 20
        ),
    )(lengths, pages, s, d, ab, v, y, c, col, z, gain)


def crowded_pages(
    u, dt_raw, wconv_x, bconv_x, wconv_bc, bconv_bc, step_bias, decay_log, lengths, pages
):
    rows = dt_raw.shape[0]
    heads = step_bias.shape[0]
    inner = wconv_x.shape[1]
    state = wconv_bc.shape[1] // 2
    taps = wconv_x.shape[0]
    prompts = lengths.shape[0]
    nseq = lax.axis_size("seq")
    base = lax.axis_index("seq") * rows
    ends = jnp.cumsum(lengths) - 1
    starts = ends - lengths + 1
    pos = base + jnp.arange(rows, dtype=jnp.int32)
    age = pos - jnp.max(jnp.where(starts[None] <= pos[:, None], starts[None], 0), axis=1)
    weight = jnp.concatenate([wconv_x, wconv_bc], axis=1)[:, : inner + state]
    total = jnp.concatenate([bconv_x, bconv_bc])[None, : inner + state]
    for k in range(taps):
        d = taps - 1 - k
        term = u[HALO - d : HALO - d + rows, : inner + state].astype(F32) * weight[k][None]
        total = total + jnp.where((age >= d)[:, None], term, 0.0)
    conv = jax.nn.silu(total).astype(BF16)
    x, b = conv[:, :inner], conv[:, inner:]
    dt = jax.nn.softplus(dt_raw[:, :heads] + step_bias[None])
    cum = jnp.cumsum(-dt * jnp.exp(decay_log)[None], axis=0)
    block = ends // rows
    before = jnp.concatenate([jnp.full((1,), -1, block.dtype), block[:-1]])
    after = jnp.concatenate([block[1:], jnp.full((1,), -1, block.dtype)])
    mine = (before == block) & (after == block) & (block == lax.axis_index("seq"))
    at_end = cum[jnp.clip(ends - base, 0, rows - 1)]
    keep = mine[:, None] & (pos[None] >= starts[:, None]) & (pos[None] <= ends[:, None])
    scale = jnp.where(
        keep[:, :, None], jnp.exp(jnp.minimum(at_end[:, None] - cum[None], 0.0)) * dt[None], 0.0
    )
    x_heads = x.reshape(rows, heads, -1).astype(F32)
    weighted = (scale[:, :, :, None] * x_heads[None]).astype(BF16).reshape(prompts, rows, inner)
    finals = jnp.einsum("rjc,jn->rcn", weighted, b, preferred_element_type=F32)
    hits = (pages[None, :] == jnp.arange(nseq, dtype=jnp.int32)[:, None]).astype(BF16)
    pool = jnp.einsum("qr,rcn->qcn", hits, finals.astype(BF16), preferred_element_type=F32)
    moved = lax.all_to_all(pool.astype(BF16), "seq", 0, 0, tiled=True)
    return jnp.sum(moved.astype(F32), axis=0)


def body(
    tokens, weight_x, weight_z, weight_bc, weight_dt, conv_x_weight, conv_x_bias,
    conv_bc_weight, conv_bc_bias, step_bias, decay_log, skip_gain, norm_gain, lengths, page_table,
):
    nseq, nhead = lax.axis_size("seq"), lax.axis_size("head")
    heads = weight_dt.shape[0]
    inner = weight_x.shape[1]
    width = inner // heads
    kept = conv_x_weight.shape[0] - 1
    u, z, dt_raw = project(tokens, weight_x, weight_z, weight_bc, weight_dt, nseq, nhead)
    s, d, ab, v, y, c, col, more = local(
        u, dt_raw, conv_x_weight, conv_x_bias[None, :], conv_bc_weight, conv_bc_bias[None, :],
        step_bias[:, None], decay_log[:, None], jnp.repeat(skip_gain, width)[None, :],
        lengths, page_table, nseq,
    )
    normed, page, conv_x, conv_bc = finish(
        s, d, ab, v, y, c, col, z, norm_gain[None, :], lengths, page_table, heads, kept,
        nseq, nhead,
    )
    page = lax.cond(
        more[0] > 0,
        lambda page, *rest: page + crowded_pages(*rest),
        lambda page, *rest: page,
        page, u, dt_raw, conv_x_weight, conv_x_bias, conv_bc_weight, conv_bc_bias, step_bias,
        decay_log, lengths, page_table,
    )
    return (
        normed, page.reshape(1, heads, width, -1), conv_x[None], conv_bc[None],
    )


def solution(mesh):
    in_specs = (
        P("seq", "head"), P(None, "head"), P(None, "head"), P(), P("head", None),
        P(None, "head"), P("head"), P(), P(), P("head"), P("head"), P("head"), P("head"),
        P(), P(),
    )
    out_specs = (
        P("seq", "head"), P("seq", "head", None, None), P("seq", None, "head"),
        P("seq", None, None),
    )
    return jax.shard_map(body, mesh=mesh, in_specs=in_specs, out_specs=out_specs, check_vma=False)
```

time: 606 us -> 78.2 us (0.13)
  blocking collectives: 228 us -> 0 us
  waiting for transfers between devices: 177 us -> 0 us
  other arithmetic: 80.3 us -> 0 us
  Pallas kernels: 0 us -> 64.5 us
  local copies, waits for them, and re-layouts: 68 us -> 11.1 us
  matrix products: 26.6 us -> 0 us
  between operations: 15.1 us -> 1.41 us
    unnamed x2 -> x0, blocking collectives: 174 us -> none
    reduce_scatter x1 -> x0, waiting for transfers between devices: 142 us -> none  [body(): lax.psum_scatter(pool_ssm.astype(jnp.bfloat16), 'seq', scatter_dimension=...]
    pallas_call x0 -> x3, Pallas kernels: none -> 64.5 us  [the longest x1 31.1 us: finish(): pl.pallas_call(functools.partial(finish_kernel, nseq, nhead, heads), name...]
    psum x1 -> x0, blocking collectives: 53.8 us -> none  [body(): square_total = lax.psum(jnp.sum(gated_out * gated_out, axis=1), 'head')]
    select_n x36 -> x0, other arithmetic: 36.7 us -> none  [the longest x31 32.7 us: step(): jnp.where(position < mine, new, old)]
    all_gather x2 -> x0, waiting for transfers between devices: 30.7 us -> none  [the longest x1 30.6 us: body(): shard_piece = lax.all_gather(tokens, 'head', axis=1, tiled=True)]
    gather x37 -> x0, local copies, waits for them, and re-layouts: 27.4 us -> none
    dot_general x15 -> x0, matrix products: 26.6 us -> none  [the longest x3 8.18 us: project(): return jnp.dot(shard_piece, matrix, preferred_element_type=jnp.float32)]
  transfers between devices with their start and end apart: 5 -> 0, of which waited for: 3 -> 0; matrix products, arithmetic and copies ran while one was open for 17% -> 0% of each run, Pallas kernels for 0% -> 0%
where the time goes in v1:
time: 78.2 us; the launch traced here: 77 us
  Pallas kernels  64.5 us (82%)
  local copies, waits for them, and re-layouts  11.1 us (14%)
  between operations  1.41 us (2%)
    pallas_call x1, Pallas kernels, finish(): pl.pallas_call(functools.partial(finish_kernel, nseq, nhead, heads), name...  31.1 us
    pallas_call x1, Pallas kernels, project(): pl.pallas_call(functools.partial(project_kernel, nseq, nhead), name='proj...  26.3 us
    unnamed x32, local copies, waits for them, and re-layouts  8.84 us
    pallas_call x1, Pallas kernels, local(): pl.pallas_call(local_kernel, name='local', out_shape=(jax.ShapeDtypeStruc...  7.14 us

profile of v1, /device:TPU:1, one launch (start us, length us, event | category | flops | bytes accessed | tf_op | source)
XLA Modules:
  0.0 77.0 jit_solution(11331769417504629401)
XLA Ops:
  0.6 0.7 broadcast_in_dim.102
  1.4 0.1 broadcast_in_dim_reshape.3.skip
  1.4 0.7 copy.48.decay_log
  2.2 0.7 copy.47.step_bias
  2.9 0.0 copy-start
  2.9 1.6 %copy-done = bf16[2048,512]{1,0:T(8,128)(2,1)S(1)} copy-done((bf16[2048,512]{1,0:T(8,128)(2,1)S(1)}, bf16[2048,512]{1,0:T(8,128)(2,1)}, u32[]{:S(2)}) %copy-start) | copy-done | bytes 2097176
  4.5 0.0 copy-start.1
  4.5 1.6 %copy-done.1 = bf16[2048,512]{1,0:T(8,128)(2,1)S(1)} copy-done((bf16[2048,512]{1,0:T(8,128)(2,1)S(1)}, bf16[2048,512]{1,0:T(8,128)(2,1)}, u32[]{:S(2)}) %copy-start.1) | copy-done | bytes 2097176
  6.1 0.0 copy-start.2
  6.1 1.2 %copy-done.2 = bf16[2048,256]{1,0:T(8,128)(2,1)S(1)} copy-done((bf16[2048,256]{1,0:T(8,128)(2,1)S(1)}, bf16[2048,256]{1,0:T(8,128)(2,1)}, u32[]{:S(2)}) %copy-start.2) | copy-done | bytes 1048600
  7.3 0.0 copy-start.3
  7.3 0.9 %copy-done.3 = bf16[512,256]{1,0:T(8,128)(2,1)S(1)} copy-done((bf16[512,256]{1,0:T(8,128)(2,1)S(1)}, bf16[512,256]{1,0:T(8,128)(2,1)}, u32[]{:S(2)}) %copy-start.3) | copy-done | bytes 262168
  8.3 0.0 copy-start.4
  8.3 0.8 copy-done.4
  9.0 0.0 copy-start.6
  9.0 0.0 copy-start.8
  9.0 0.0 copy-start.9
  9.0 0.0 copy-start.12
  9.0 0.0 copy-start.15
  9.0 0.0 copy-start.16
  9.0 0.0 copy-start.5
  9.1 26.3 %project.1 = (bf16[528,768]{1,0:T(8,128)(2,1)S(1)}, bf16[512,512]{1,0:T(8,128)(2,1)S(1)}, f32[512,128]{1,0:T(8,128)S(1)}) custom-call(bf16[512,256]{1,0:T(8,128)(2,1)S(1)} %copy-done.3, bf16[2048,512]{1,0:T(8,128)(2,1)S(1)} %copy-done, bf16[2048,512]{1,0:T(8,128)(2,1)S(1)} %copy-done.1, bf16[2048,256]{1,0:T(8,128)(2,1)S(1)} %copy-done.2, ...), custom_call_target="tpu_custom_call" | custom-call | tf_op jit(solution)/shard_map/project/pallas_call | solution.py:200
  35.3 0.0 copy-done.6
  35.3 0.0 copy-done.8
  35.3 0.0 copy-done.9
  35.4 0.0 copy-done.12
  35.4 0.0 copy-done.15
  35.4 0.0 copy-done.16
  35.4 7.1 %local.1 = (bf16[32,16,128]{2,1,0:T(8,128)(2,1)S(1)}, f32[4,2,128]{2,1,0:T(2,128)S(1)}, bf16[32,2,16,128]{3,2,1,0:T(8,128)(2,1)S(1)}, bf16[32,32,128]{2,1,0:T(8,...) custom-call(s32[8]{0:T(128)S(1)} %copy-done.15, ...), custom_call_target="tpu_custom_call" | custom-call | tf_op jit(solution)/shard_map/local/pallas_call | solution.py:455
  43.2 0.0 copy-done.5
  43.2 0.0 copy-start.17
  43.2 0.0 copy-start.18
  43.2 31.1 %finish.1 = (bf16[512,512]{1,0:T(8,128)(2,1)S(1)}, f32[512,128]{1,0:T(8,128)S(1)}, f32[3,512]{1,0:T(4,128)S(1)}, f32[3,256]{1,0:T(4,128)S(1)}) custom-call(s32[8]{0:T(128)S(1)} %copy-done.15, s32[8]{0:T(128)S(1)} %copy-done.12, bf16[32,16,128]{2,1,0:T(8,128)(2,1)S(1)} %get-tuple-element.64.s_in, f32[4,2,128]{2,1,0:T(2,128)S(1)} %get-tuple-element.65.d_in, ...), custom_call_target="tpu_custom_call" | custom-call | tf_op jit(solution)/shard_map/finish/pallas_call | solution.py:688
  74.3 0.6 copy.51
  74.9 0.6 copy.50
  75.5 0.0 copy-done.17
  75.5 0.0 copy-done.18
  75.5 0.8 %copy.65 = bf16[512,512]{1,0:T(8,128)(2,1)} copy(bf16[512,512]{1,0:T(8,128)(2,1)S(1)} %get-tuple-element.162) | data formatting | bytes 1048576
  76.3 0.7 copy.66
  (1 shorter events, 0.0 us)
Async XLA Ops:
  2.9 1.6 %copy-start = (bf16[2048,512]{1,0:T(8,128)(2,1)S(1)}, bf16[2048,512]{1,0:T(8,128)(2,1)}, u32[]{:S(2)}) copy-start(bf16[2048,512]{1,0:T(8,128)(2,1)} %wx.1) | copy-start | bytes 6291460
  4.5 1.6 %copy-start.1 = (bf16[2048,512]{1,0:T(8,128)(2,1)S(1)}, bf16[2048,512]{1,0:T(8,128)(2,1)}, u32[]{:S(2)}) copy-start(bf16[2048,512]{1,0:T(8,128)(2,1)} %wz.1) | copy-start | bytes 6291460
  6.1 1.2 %copy-start.2 = (bf16[2048,256]{1,0:T(8,128)(2,1)S(1)}, bf16[2048,256]{1,0:T(8,128)(2,1)}, u32[]{:S(2)}) copy-start(bf16[2048,256]{1,0:T(8,128)(2,1)} %wbc.1) | copy-start | bytes 3145732
  7.3 0.9 %copy-start.3 = (bf16[512,256]{1,0:T(8,128)(2,1)S(1)}, bf16[512,256]{1,0:T(8,128)(2,1)}, u32[]{:S(2)}) copy-start(bf16[512,256]{1,0:T(8,128)(2,1)} %tok.1) | copy-start | bytes 786436
  8.3 0.8 copy-start.4
  9.0 26.3 %copy-start.6 = (f32[4,512]{1,0:T(4,128)S(1)}, f32[4,512]{1,0:T(4,128)}, u32[]{:S(2)}) copy-start(f32[4,512]{1,0:T(4,128)} %wconv_x.1) | copy-start | bytes 24580
  9.0 26.3 %copy-start.8 = (f32[4,256]{1,0:T(4,128)S(1)}, f32[4,256]{1,0:T(4,128)}, u32[]{:S(2)}) copy-start(f32[4,256]{1,0:T(4,128)} %wconv_bc.1) | copy-start | bytes 12292
  9.0 26.3 %copy-start.9 = (f32[512]{0:T(512)S(1)}, f32[512]{0:T(512)}, u32[]{:S(2)}) copy-start(f32[512]{0:T(512)} %param.23) | copy-start | bytes 6148
  9.0 26.3 %copy-start.12 = (s32[8]{0:T(128)S(1)}, s32[8]{0:T(128)}, u32[]{:S(2)}) copy-start(s32[8]{0:T(128)} %page_ref.3) | copy-start | bytes 100
  9.0 26.3 %copy-start.15 = (s32[8]{0:T(128)S(1)}, s32[8]{0:T(128)}, u32[]{:S(2)}) copy-start(s32[8]{0:T(128)} %len_ref.3) | copy-start | bytes 100
  9.0 26.3 %copy-start.16 = (f32[256]{0:T(256)S(1)}, f32[256]{0:T(256)}, u32[]{:S(2)}) copy-start(f32[256]{0:T(256)} %param.25) | copy-start | bytes 3076
  9.0 34.1 %copy-start.5 = (f32[512]{0:T(512)S(1)}, f32[512]{0:T(512)}, u32[]{:S(2)}) copy-start(f32[512]{0:T(512)} %param.29) | copy-start | bytes 6148
  43.2 32.3 %copy-start.17 = (f32[8]{0:T(128)S(1)}, f32[8]{0:T(128)}, u32[]{:S(2)}) copy-start(f32[8]{0:T(128)} %param.26) | copy-start | bytes 100
  43.2 32.3 %copy-start.18 = (f32[8]{0:T(128)S(1)}, f32[8]{0:T(128)}, u32[]{:S(2)}) copy-start(f32[8]{0:T(128)} %param.27) | copy-start | bytes 100

commit v2 on v1

v2 whole, which is shorter than its diff:
```python
import functools

import jax
import jax.numpy as jnp
from jax import lax
from jax.experimental import pallas as pl
from jax.experimental.pallas import tpu as pltpu
from jax.sharding import PartitionSpec as P

MESH = pl.DeviceIdType.MESH
F32 = jnp.float32
BF16 = jnp.bfloat16
EPS = 1e-05
HALO = 16
PROJECT_VMEM = (60 << 20) + (1 << 19)
LOG2E = 1.4426950408889634


def vmem():
    return pl.BlockSpec(memory_space=pltpu.VMEM)


def hbm():
    return pl.BlockSpec(memory_space=pltpu.HBM)


def smem():
    return pl.BlockSpec(memory_space=pltpu.SMEM)


def project_kernel(
    nseq, nhead,
    tok, wx, wz, wbc, wdt,
    acc, accdt,
    tokbuf, w, wdtp,
    lsem, ssem, rsem, hs_sem, hr_sem,
):
    ny = nhead // 2
    seq = lax.axis_index("seq")
    head = lax.axis_index("head")
    y = head // 2
    core = head % 2
    rows, feat = tok.shape
    half = rows // 2
    inner = wx.shape[1]
    wide = wbc.shape[1]
    heads = wdt.shape[0]
    yp, ym = (y + 1) % ny, (y + ny - 1) % ny
    y2 = (y + 2) % ny
    up, down = yp * 2 + core, ym * 2 + core
    other = y * 2 + (1 - core)
    nxt, prv = (seq + 1) % nseq, (seq + nseq - 1) % nseq
    lanes = pl.ds(pl.multiple_of(core * feat, feat), feat)
    other_lanes = pl.ds(pl.multiple_of((1 - core) * feat, feat), feat)
    first, second = pl.ds(HALO, half), pl.ds(HALO + half, half)
    both = pl.ds(HALO, rows)
    edge = pl.ds(0, HALO)

    loads = [
        pltpu.make_async_copy(tok, tokbuf.at[y, both, lanes], lsem.at[0]),
        pltpu.make_async_copy(wx, w.at[:, pl.ds(0, inner)], lsem.at[1]),
        pltpu.make_async_copy(wbc, w.at[:, pl.ds(2 * inner, wide)], lsem.at[2]),
        pltpu.make_async_copy(wz, w.at[:, pl.ds(inner, inner)], lsem.at[3]),
        pltpu.make_async_copy(wdt, wdtp.at[pl.ds(0, heads)], lsem.at[4]),
    ]

    barrier = pltpu.get_barrier_semaphore()
    for k in range(1, nhead):
        pl.semaphore_signal(
            barrier, inc=1, device_id={"head": (head + k) % nhead}, device_id_type=MESH
        )
    pl.semaphore_signal(barrier, inc=1, device_id={"seq": nxt}, device_id_type=MESH)
    pl.semaphore_signal(barrier, inc=1, device_id={"seq": prv}, device_id_type=MESH)
    wdtp[pl.ds(heads, 128 - heads), :] = jnp.zeros((128 - heads, wdtp.shape[1]), BF16)
    for one in loads:
        one.start()
    pl.semaphore_wait(barrier, nhead + 1)

    sent = []

    def send(src, dst, number, to):
        copy = pltpu.make_async_remote_copy(
            src_ref=src, dst_ref=dst, send_sem=ssem.at[number], recv_sem=rsem.at[number],
            device_id=to, device_id_type=MESH,
        )
        copy.start()
        sent.append(copy)

    def arrive(region, number):
        pltpu.make_async_remote_copy(
            src_ref=region, dst_ref=region, send_sem=ssem.at[number], recv_sem=rsem.at[number],
            device_id={"head": other}, device_id_type=MESH,
        ).wait_recv()

    to_up, to_down, to_other = {"head": up}, {"head": down}, {"head": other}
    mine = tokbuf.at[y]
    send(tok.at[pl.ds(rows - HALO, HALO)], mine.at[edge, lanes], 13, {"seq": nxt})
    send(tok.at[pl.ds(0, half)], mine.at[first, lanes], 1, to_up)
    send(tok.at[pl.ds(half, half)], mine.at[second, lanes], 3, to_down)
    send(tok, mine.at[both, lanes], 0, to_other)
    send(tok.at[pl.ds(half, half)], mine.at[second, lanes], 2, to_up)
    send(tok.at[pl.ds(0, half)], mine.at[first, lanes], 4, to_down)

    def halo_piece(owner):
        return tokbuf.at[
            owner // 2, edge, pl.ds(pl.multiple_of((owner % 2) * feat, feat), feat)
        ]

    arrive(halo_piece(head), 13)
    halo_sends = []
    for k in range(1, nhead):
        copy = pltpu.make_async_remote_copy(
            src_ref=halo_piece(head), dst_ref=halo_piece(head),
            send_sem=hs_sem.at[k], recv_sem=hr_sem.at[head],
            device_id={"head": (head + k) % nhead}, device_id_type=MESH,
        )
        copy.start()
        halo_sends.append(copy)

    def halo_arrive(owner):
        pltpu.make_async_remote_copy(
            src_ref=halo_piece(owner), dst_ref=halo_piece(owner),
            send_sem=hs_sem.at[0], recv_sem=hr_sem.at[owner],
            device_id={"head": other}, device_id_type=MESH,
        ).wait_recv()

    tile = 256
    tiles = (2 * inner + wide) // tile

    def multiply(at, start):
        k = pl.ds(pl.multiple_of(at * 2 * feat, 2 * feat), 2 * feat)

        @pl.loop(0, tiles)
        def _(n):
            cols = pl.ds(pl.multiple_of(n * tile, tile), tile)
            part = jnp.dot(tokbuf[at], w[k, cols], preferred_element_type=F32)
            if start:
                acc[:, cols] = part
            else:
                acc[:, cols] += part

        part = lax.dot_general(
            tokbuf[at, both, :], wdtp[:, k], (((1,), (1,)), ((), ())),
            preferred_element_type=F32,
        )
        if start:
            accdt[...] = part
        else:
            accdt[...] += part

    for one in loads:
        one.wait()
    arrive(mine.at[both, other_lanes], 0)
    halo_arrive(other)
    multiply(y, True)

    arrive(tokbuf.at[ym, first, lanes], 1)
    send(tokbuf.at[ym, first, lanes], tokbuf.at[ym, first, lanes], 5, to_up)
    arrive(tokbuf.at[yp, second, lanes], 3)
    send(tokbuf.at[yp, second, lanes], tokbuf.at[yp, second, lanes], 6, to_down)
    send(tokbuf.at[ym, first, lanes], tokbuf.at[ym, first, lanes], 7, to_other)
    send(tokbuf.at[yp, second, lanes], tokbuf.at[yp, second, lanes], 9, to_other)
    arrive(tokbuf.at[ym, second, lanes], 2)
    send(tokbuf.at[ym, second, lanes], tokbuf.at[ym, second, lanes], 8, to_other)
    arrive(tokbuf.at[yp, first, lanes], 4)
    send(tokbuf.at[yp, first, lanes], tokbuf.at[yp, first, lanes], 10, to_other)
    arrive(tokbuf.at[ym, first, other_lanes], 7)
    arrive(tokbuf.at[ym, second, other_lanes], 8)
    halo_arrive(ym * 2)
    halo_arrive(ym * 2 + 1)
    multiply(ym, False)
    arrive(tokbuf.at[yp, second, other_lanes], 9)
    arrive(tokbuf.at[yp, first, other_lanes], 10)
    halo_arrive(yp * 2)
    halo_arrive(yp * 2 + 1)
    multiply(yp, False)

    arrive(tokbuf.at[y2, first, lanes], 5)
    send(tokbuf.at[y2, first, lanes], tokbuf.at[y2, first, lanes], 11, to_other)
    arrive(tokbuf.at[y2, second, lanes], 6)
    send(tokbuf.at[y2, second, lanes], tokbuf.at[y2, second, lanes], 12, to_other)
    halo_arrive(y2 * 2)
    halo_arrive(y2 * 2 + 1)
    arrive(tokbuf.at[y2, first, other_lanes], 11)
    arrive(tokbuf.at[y2, second, other_lanes], 12)
    multiply(y2, False)

    for copy in sent + halo_sends:
        copy.wait_send()


def project(tokens, weight_x, weight_z, weight_bc, weight_dt, nseq, nhead, interpret=False):
    rows, feat = tokens.shape
    depth, inner = weight_x.shape
    wide = weight_bc.shape[1]
    total = 2 * inner + wide
    return pl.pallas_call(
        functools.partial(project_kernel, nseq, nhead),
        name="project",
        out_shape=(
            jax.ShapeDtypeStruct((rows + HALO, total), F32),
            jax.ShapeDtypeStruct((rows, 128), F32),
        ),
        in_specs=[hbm()] * 5,
        out_specs=(vmem(), vmem()),
        scratch_shapes=[
            pltpu.VMEM((nhead // 2, rows + HALO, 2 * feat), BF16),
            pltpu.VMEM((depth, total), BF16),
            pltpu.VMEM((128, depth), BF16),
            pltpu.SemaphoreType.DMA((5,)),
            pltpu.SemaphoreType.DMA((14,)),
            pltpu.SemaphoreType.DMA((14,)),
            pltpu.SemaphoreType.DMA((nhead,)),
            pltpu.SemaphoreType.DMA((nhead,)),
        ],
        compiler_params=pltpu.CompilerParams(
            collective_id=0, has_side_effects=True, vmem_limit_bytes=PROJECT_VMEM
        ),
    )(tokens, weight_x, weight_z, weight_bc, weight_dt)


def silu(x):
    half = 0.5 * x
    return half + half * jnp.tanh(half)


def read_prompts(len_ref, count):
    starts, ends = [], []
    at = jnp.int32(0)
    for r in range(count):
        starts.append(at)
        at = at + len_ref[r]
        ends.append(at - 1)
    return starts, ends


def ends_in_block(starts, ends, base, rows):
    count = len(starts)
    none = jnp.int32(-1)
    a_start, a_end = none, none
    b_start, b_end = none, none
    a_at = none
    for r in range(count - 1, -1, -1):
        here = (ends[r] >= base) & (ends[r] < base + rows)
        a_start = jnp.where(here, starts[r], a_start)
        a_end = jnp.where(here, ends[r], a_end)
        a_at = jnp.where(here, r, a_at)
    for r in range(count):
        here = (ends[r] >= base) & (ends[r] < base + rows) & (a_at != r)
        b_start = jnp.where(here, starts[r], b_start)
        b_end = jnp.where(here, ends[r], b_end)
    return a_start, a_end, b_start, b_end


def end_slots(starts, ends, rows):
    prompts = len(starts)
    slot, block = [], []
    for r in range(prompts):
        at = ends[r] // rows
        a = jnp.bool_(True) if r == 0 else (ends[r - 1] // rows) != at
        b = jnp.bool_(True) if r == prompts - 1 else (ends[r + 1] // rows) != at
        slot.append(jnp.where(a, 0, jnp.where(b, 1, 2)).astype(jnp.int32))
        block.append(at)
    return slot, block


def by_head(values, shape):
    which = lax.broadcasted_iota(jnp.int32, shape, 0)
    out = jnp.zeros(shape, F32)
    for h in range(shape[0]):
        out = jnp.where(which == h, values[h], out)
    return out


def block_kernel(
    xs, zs, nhead,
    len_ref, page_ref, step_bias, decay_log, skip_gain,
    u, dt_raw, wconv_x, bconv_x, wconv_bc, bconv_bc,
    gated, scale_out, page_out, v_out, more_out,
    xc, bcol, ccol, btr, scores, cols, stage, y_loc,
    s_send, d_send, ab_send, v_all, v_send, s_buf, d_buf, ab_buf, v_buf,
    h_all, h_send, h_buf, p_send, q_send, q_buf, where_ref,
    send_sem, recv_sem, qs_sem, qr_sem,
):
    nseq = xs * zs
    seq = lax.axis_index("seq")
    head = lax.axis_index("head")
    my_x, my_z = seq // zs, seq % zs
    rows, inner = xc.shape
    state = ccol.shape[1]
    heads = step_bias.shape[0]
    lbs = inner // 128
    per = nseq // lbs
    piece = state // per
    prompts = len_ref.shape[0]
    taps = wconv_x.shape[0]
    lb_me = seq // per
    base = seq * rows

    barrier = pltpu.get_barrier_semaphore()

    @pl.loop(1, nseq)
    def _(d):
        pl.semaphore_signal(
            barrier, inc=1, device_id={"seq": (seq + d) % nseq}, device_id_type=MESH
        )

    for k in range(1, nhead):
        pl.semaphore_signal(
            barrier, inc=1, device_id={"head": (head + k) % nhead}, device_id_type=MESH
        )

    starts, ends = read_prompts(len_ref, prompts)
    slot, block = end_slots(starts, ends, rows)
    more = jnp.int32(0)
    for kind in slot:
        more = jnp.maximum(more, kind - 1)
    more_out[0] = more

    def start_of(pos):
        found = jnp.zeros_like(pos)
        for r in range(prompts):
            found = jnp.where(starts[r] <= pos, starts[r], found)
        return found

    dtr = jnp.transpose(dt_raw[...])[0:heads, :]
    pre = dtr + by_head(step_bias, (heads, rows))
    dt = jnp.maximum(pre, 0.0) + jnp.log1p(jnp.exp(-jnp.abs(pre)))
    cum = -dt * jnp.exp(by_head(decay_log, (heads, rows)))
    lane = lax.broadcasted_iota(jnp.int32, (heads, rows), 1)
    shift = 1
    while shift < rows:
        cum = cum + jnp.where(lane >= shift, pltpu.roll(cum, shift, 1), 0.0)
        shift *= 2
    pos = base + lane
    start_row = start_of(pos)
    a_start, a_end, b_start, b_end = ends_in_block(starts, ends, base, rows)
    last_start = start_of(jnp.full((heads, rows), base + rows - 1, jnp.int32))

    def at_pos(where_pos):
        return jnp.sum(jnp.where(pos == where_pos, cum, 0.0), axis=1, keepdims=True)

    cum_last = at_pos(base + rows - 1)
    cum_a, cum_b = at_pos(a_end), at_pos(b_end)

    def weight_to(cum_end, keep):
        return jnp.where(keep, jnp.exp(jnp.minimum(cum_end - cum, 0.0)), 0.0) * dt

    w_end = weight_to(cum_last, pos >= last_start)
    w_a = weight_to(cum_a, (pos >= a_start) & (pos <= a_end))
    w_b = weight_to(cum_b, (pos >= b_start) & (pos <= b_end))
    inflow = jnp.where(start_row < base, jnp.exp(cum), 0.0)
    decay = jnp.where(last_start[:, 0:1] < base, jnp.exp(cum_last), 0.0)
    decay_a = jnp.where(
        (jnp.full((heads, 1), a_start) < base) & (jnp.full((heads, 1), a_end) >= 0),
        jnp.exp(cum_a), 0.0,
    )
    cum2 = cum * LOG2E
    age_row = (pos - start_row).astype(F32)
    packed = jnp.concatenate(
        [cum2, inflow, w_end, w_a, w_b, age_row]
        + [jnp.zeros((128 - 6 * heads, rows), F32)], axis=0,
    )
    cols[...] = jnp.transpose(packed)
    low_row = lax.broadcasted_iota(jnp.int32, (1, 128), 1) < 64

    for lb in range(lbs):
        h0, h1 = 2 * lb, 2 * lb + 1
        for k, value in enumerate((decay, decay_a)):
            d_send[lb, pl.ds(k, 1), :] = jnp.where(
                low_row,
                jnp.broadcast_to(value[h0 : h0 + 1, :], (1, 128)),
                jnp.broadcast_to(value[h1 : h1 + 1, :], (1, 128)),
            )

    step = 64

    @pl.loop(0, rows // step)
    def _(t):
        r0 = pl.multiple_of(t * step, step)
        age = jnp.broadcast_to(cols[pl.ds(r0, step), 5 * heads : 5 * heads + 1], (step, 128))
        near = [age >= d for d in range(taps)]
        for j in range(lbs + 2):
            lanes = pl.ds(j * 128, 128)
            win = u[pl.ds(r0, step + HALO), pl.ds((j if j < lbs else j + lbs) * 128, 128)]
            if j < lbs:
                wl, wt, wb = lanes, wconv_x, bconv_x
            else:
                wl, wt, wb = pl.ds((j - lbs) * 128, 128), wconv_bc, bconv_bc
            total = jnp.broadcast_to(wb[:, wl], (step, 128))
            for k in range(taps):
                d = taps - 1 - k
                shifted = win if d == 0 else pltpu.roll(win, d, 0)
                term = shifted[HALO:, :] * wt[pl.ds(k, 1), wl]
                total = total + (term if d == 0 else jnp.where(near[d], term, 0.0))
            out = silu(total)
            if j < lbs:
                xc[pl.ds(r0, step), lanes] = out.astype(BF16)
            elif j == lbs:
                bcol[pl.ds(r0, step), :] = out.astype(BF16).astype(F32)
            else:
                ccol[pl.ds(r0, step), :] = out.astype(BF16)

    btr[...] = jnp.transpose(bcol[...]).astype(BF16)

    low = lax.broadcasted_iota(jnp.int32, (rows, 128), 1) < 64

    def state_of(kind, lb):
        at = (2 + kind) * heads + 2 * lb
        scale = jnp.where(low, cols[:, at : at + 1], cols[:, at + 1 : at + 2])
        weighted = (xc[:, pl.ds(lb * 128, 128)].astype(F32) * scale).astype(BF16)
        value = jnp.dot(btr[...], weighted, preferred_element_type=F32)
        return value.astype(BF16).reshape(per, piece, 128)

    for lb in range(lbs):
        s_send[pl.ds(lb * per, per)] = state_of(0, lb)
    pl.semaphore_wait(barrier, nseq - 1 + nhead - 1)

    S, D, AB, V, H, PG = range(6)

    def offset(n):
        t, s = n // xs, n % xs
        dz = (zs // 2 + (1 - 2 * (t % 2)) * ((t + 1) // 2)) % zs
        dx = (xs // 2 + (1 - 2 * (s % 2)) * ((s + 1) // 2)) % xs
        return dx, dz

    def copy(kind, src, dst, n, to):
        return pltpu.make_async_remote_copy(
            src_ref=src, dst_ref=dst, send_sem=send_sem.at[kind, n], recv_sem=recv_sem.at[kind, n],
            device_id={"seq": to}, device_id_type=MESH,
        )

    def out_copy(kind, n):
        dx, dz = offset(n)
        to = ((my_x + dx) % xs) * zs + (my_z + dz) % zs
        if kind == S:
            return copy(S, s_send.at[to], s_buf.at[seq], n, to)
        if kind == D:
            return copy(D, d_send.at[to // per], d_buf.at[seq], n, to)
        if kind == AB:
            return copy(AB, ab_send.at[to], ab_buf.at[seq], n, to)
        if kind == V:
            return copy(V, v_send.at[to], v_buf.at[seq], n, to)
        if kind == H:
            return copy(H, h_send.at[to], h_buf.at[seq], n, to)
        return copy(PG, p_send.at[to], page_out.at[seq], n, to)

    def in_copy(kind, n):
        dx, dz = offset(n)
        frm = ((my_x + xs - dx) % xs) * zs + (my_z + zs - dz) % zs
        buf = (s_buf, d_buf, ab_buf, v_buf, h_buf, page_out)[kind]
        return copy(kind, buf.at[frm], buf.at[frm], n, frm)

    def start_all(*kinds):
        @pl.loop(0, nseq - 1)
        def _(n):
            for kind in kinds:
                out_copy(kind, n).start()

    def arrive_all(*kinds):
        @pl.loop(0, nseq - 1)
        def _(n):
            for kind in kinds:
                in_copy(kind, n).wait_recv()

    start_all(S, D)
    for lb in range(lbs):
        for kind in range(2):
            ab_send[pl.ds(lb * per, per), kind] = state_of(1 + kind, lb)
    start_all(AB)
    s_buf[seq] = s_send[seq]
    d_buf[seq] = d_send[lb_me]
    ab_buf[seq] = ab_send[seq]

    tile = 128
    blocks = rows // tile
    for i in range(blocks):
        ri = pl.ds(i * tile, tile)
        reach = (i + 1) * tile
        sc = jnp.dot(ccol[ri, :], btr[:, 0:reach], preferred_element_type=F32)
        gap_i = i * tile + lax.broadcasted_iota(jnp.int32, (tile, reach), 0)
        gap_j = lax.broadcasted_iota(jnp.int32, (tile, reach), 1)
        back = (gap_i - gap_j).astype(F32)
        age = cols[ri, 5 * heads : 5 * heads + 1]
        scores[ri, 0:reach] = jnp.where((back >= 0.0) & (back <= age), sc, 0.0)
    low_t = lax.broadcasted_iota(jnp.int32, (tile, 128), 1) < 64
    for lb in range(lbs):
        lanes = pl.ds(lb * 128, 128)
        gain = jnp.where(low_row, skip_gain[2 * lb], skip_gain[2 * lb + 1])
        for i in range(blocks):
            ri = pl.ds(i * tile, tile)
            reach = (i + 1) * tile
            parts = []
            for hh in range(2):
                h = 2 * lb + hh
                gap = jnp.minimum(cols[ri, h : h + 1] - cum2[h : h + 1, 0:reach], 0.0)
                wgt = (scores[ri, 0:reach] * jnp.exp2(gap) * dt[h : h + 1, 0:reach]).astype(BF16)
                parts.append(jnp.dot(wgt, xc[0:reach, lanes], preferred_element_type=F32))
            y_loc[ri, lanes] = (
                jnp.where(low_t, parts[0], parts[1]) + gain * xc[ri, lanes].astype(F32)
            )

    arrive_all(S, D)

    def advance(i, carried):
        h_all[i] = carried
        h_send[i] = carried.astype(BF16)
        return d_buf[i, 0:1, :] * carried + s_buf[i].astype(F32)

    lax.fori_loop(0, nseq, advance, jnp.zeros((piece, 128), F32))
    start_all(H)
    h_buf[seq] = h_send[seq]

    @pl.loop(0, nseq)
    def _(q):
        kind = jnp.int32(2)
        at = jnp.int32(0)
        who = jnp.int32(prompts)
        for r in range(prompts):
            hit = page_ref[r] == q
            kind = jnp.where(hit, slot[r], kind)
            at = jnp.where(hit, block[r], at)
            who = jnp.where(hit & (block[r] == seq), r, who)
        where_ref[0, q] = kind
        where_ref[1, q] = jnp.clip(at, 0, nseq - 1)
        where_ref[2, q] = who

    v_rows = v_all.shape[1]
    v_all[prompts] = jnp.zeros((v_rows, 128), BF16)
    for r in range(prompts):
        local = jnp.clip(ends[r] - base, 0, rows - 1) + HALO
        for k in range(taps - 1):
            back = taps - 2 - k
            line = u[pl.ds(local - back, 1), :]
            keep = jnp.full((1, 128), ends[r] - back, jnp.int32) >= starts[r]
            for j in range(lbs):
                stage[k * lbs + j : k * lbs + j + 1, :] = jnp.where(
                    keep, line[:, j * 128 : (j + 1) * 128], 0.0
                )
            for j in range(2):
                at = (taps - 1) * lbs + 2 * k + j
                stage[at : at + 1, :] = jnp.where(
                    keep, line[:, (2 * lbs + j) * 128 : (2 * lbs + j + 1) * 128], 0.0
                )
        v_all[r] = stage[...].astype(BF16)

    @pl.loop(0, nseq)
    def _(q):
        v_send[q] = v_all[where_ref[2, q]]

    arrive_all(AB)

    @pl.loop(0, nseq)
    def _(q):
        kind = where_ref[0, q]
        at = where_ref[1, q]
        value = ab_buf[at, jnp.where(kind == 1, 1, 0)].astype(F32)
        first = value + d_buf[at, 1:2, :] * h_all[at]
        kinds = jnp.full((piece, 128), kind, jnp.int32)
        p_send[q] = jnp.where(kinds == 0, first, jnp.where(kinds == 1, value, 0.0)).astype(BF16)

    start_all(PG)
    start_all(V)
    page_out[seq] = p_send[seq]
    v_buf[seq] = v_send[seq]

    arrive_all(H)
    tile = 64
    low = lax.broadcasted_iota(jnp.int32, (tile, 128), 1) < 64
    lanes128 = lax.broadcasted_iota(jnp.int32, (tile, 128), 1)
    subl = lax.broadcasted_iota(jnp.int32, (tile, 128), 0)
    for g in range(rows // 128):
        line = jnp.zeros((1, 128), F32)
        for s in range(128 // tile):
            ri = pl.ds(g * 128 + s * tile, tile)
            total = jnp.zeros((tile, 128), F32)
            for lb in range(lbs):
                lanes = pl.ds(lb * 128, 128)
                hmat = h_buf[pl.ds(lb * per, per)].reshape(state, 128)
                ac = jnp.dot(ccol[ri, :], hmat, preferred_element_type=F32)
                at = heads + 2 * lb
                scale = jnp.where(low, cols[ri, at : at + 1], cols[ri, at + 1 : at + 2])
                yv = (y_loc[ri, lanes] + ac * scale).astype(BF16).astype(F32)
                zv = u[pl.ds(HALO + g * 128 + s * tile, tile), pl.ds(inner + lb * 128, 128)]
                gv = yv * silu(zv)
                gated[ri, lanes] = gv
                total = total + gv * gv
            col = jnp.sum(total, axis=1, keepdims=True)
            line = line + jnp.sum(
                jnp.where(lanes128 == subl + s * tile, col, 0.0), axis=0, keepdims=True
            )
        q_send[g : g + 1, :] = line

    q_copies = []
    for k in range(1, nhead):
        one = pltpu.make_async_remote_copy(
            src_ref=q_send, dst_ref=q_buf.at[head], send_sem=qs_sem.at[k], recv_sem=qr_sem.at[k],
            device_id={"head": (head + k) % nhead}, device_id_type=MESH,
        )
        one.start()
        q_copies.append(one)
    q_buf[head] = q_send[...]

    source = jnp.int32(0)
    found = jnp.int32(0)
    for r in range(prompts):
        hit = page_ref[r] == seq
        source = jnp.where(hit, block[r], source)
        found = jnp.where(hit, 1, found)
    source = jnp.clip(source, 0, nseq - 1)
    arrive_all(V)
    v_out[...] = jnp.where(
        jnp.full(v_out.shape, found, jnp.int32) == 1, v_buf[source].astype(F32), 0.0
    )

    for k in range(1, nhead):
        frm = (head + nhead - k) % nhead
        pltpu.make_async_remote_copy(
            src_ref=q_send, dst_ref=q_buf.at[frm], send_sem=qs_sem.at[k], recv_sem=qr_sem.at[k],
            device_id={"head": frm}, device_id_type=MESH,
        ).wait_recv()
    squares = q_buf[0]
    for k in range(1, nhead):
        squares = squares + q_buf[k]
    scale_out[...] = lax.rsqrt(squares / (inner * nhead) + EPS)
    arrive_all(PG)

    @pl.loop(0, nseq - 1)
    def _(n):
        for kind in (S, D, AB, V, H, PG):
            out_copy(kind, n).wait_send()

    for one in q_copies:
        one.wait_send()


def run_block(u, dt_raw, wconv_x, bconv_x, wconv_bc, bconv_bc, step_bias, decay_log, skip,
              lengths, pages, nseq, nhead):
    rows, inner = dt_raw.shape[0], wconv_x.shape[1]
    state = wconv_bc.shape[1] // 2
    lbs = inner // 128
    piece = state * lbs // nseq
    prompts = lengths.shape[0]
    xs = 4
    tiles = (nseq, piece, 128)
    v_rows = 24
    return pl.pallas_call(
        functools.partial(block_kernel, xs, nseq // xs, nhead),
        name="block",
        out_shape=(
            jax.ShapeDtypeStruct((rows, inner), F32),
            jax.ShapeDtypeStruct((rows // 128, 128), F32),
            jax.ShapeDtypeStruct(tiles, BF16),
            jax.ShapeDtypeStruct((v_rows, 128), F32),
            jax.ShapeDtypeStruct((1,), jnp.int32),
        ),
        in_specs=[smem()] * 5 + [vmem()] * 6,
        out_specs=(vmem(),) * 4 + (smem(),),
        scratch_shapes=[
            pltpu.VMEM((rows, inner), BF16),
            pltpu.VMEM((rows, state), F32),
            pltpu.VMEM((rows, state), BF16),
            pltpu.VMEM((state, rows), BF16),
            pltpu.VMEM((rows, rows), F32),
            pltpu.VMEM((rows, 128), F32),
            pltpu.VMEM((v_rows, 128), F32),
            pltpu.VMEM((rows, inner), F32),
            pltpu.VMEM(tiles, BF16),
            pltpu.VMEM((lbs, 2, 128), F32),
            pltpu.VMEM((nseq, 2, piece, 128), BF16),
            pltpu.VMEM((prompts + 1, v_rows, 128), BF16),
            pltpu.VMEM((nseq, v_rows, 128), BF16),
            pltpu.VMEM(tiles, BF16),
            pltpu.VMEM((nseq, 2, 128), F32),
            pltpu.VMEM((nseq, 2, piece, 128), BF16),
            pltpu.VMEM((nseq, v_rows, 128), BF16),
            pltpu.VMEM(tiles, F32),
            pltpu.VMEM(tiles, BF16),
            pltpu.VMEM(tiles, BF16),
            pltpu.VMEM(tiles, BF16),
            pltpu.VMEM((rows // 128, 128), F32),
            pltpu.VMEM((nhead, rows // 128, 128), F32),
            pltpu.SMEM((3, nseq), jnp.int32),
            pltpu.SemaphoreType.DMA((6, nseq)),
            pltpu.SemaphoreType.DMA((6, nseq)),
            pltpu.SemaphoreType.DMA((nhead,)),
            pltpu.SemaphoreType.DMA((nhead,)),
        ],
        compiler_params=pltpu.CompilerParams(
            collective_id=1, has_side_effects=True, vmem_limit_bytes=40 << 20
        ),
    )(lengths, pages, step_bias, decay_log, skip, u, dt_raw, wconv_x, bconv_x, wconv_bc,
      bconv_bc)


def write_kernel(gated, scale_rows, pages, v, gain, n_out, page_out, cx_out, cb_out):
    rows, inner = gated.shape
    lbs = inner // 128
    per = pages.shape[0] // lbs
    state = per * pages.shape[1]
    tile = 64
    lanes128 = lax.broadcasted_iota(jnp.int32, (tile, 128), 1)
    subl = lax.broadcasted_iota(jnp.int32, (tile, 128), 0)
    for g in range(rows // 128):
        for s in range(128 // tile):
            ri = pl.ds(g * 128 + s * tile, tile)
            diag = jnp.where(lanes128 == subl + s * tile, scale_rows[g : g + 1, :], 0.0)
            scale = jnp.sum(diag, axis=1, keepdims=True)
            n_out[ri, :] = (gated[ri, :] * scale * gain[...]).astype(BF16)
    for lb in range(lbs):
        mat = pages[pl.ds(lb * per, per)].reshape(state, 128).astype(F32)
        page_out[pl.ds(lb * 128, 128), :] = jnp.transpose(mat)
    kept = cx_out.shape[0]
    for k in range(kept):
        for j in range(lbs):
            cx_out[k, :, j * 128 : (j + 1) * 128] = v[k * lbs + j : k * lbs + j + 1, :]
        for j in range(2):
            at = kept * lbs + 2 * k + j
            cb_out[k, :, j * 128 : (j + 1) * 128] = v[at : at + 1, :]


def write(gated, scale_rows, pages, v, gain, state, kept):
    rows, inner = gated.shape
    return pl.pallas_call(
        write_kernel,
        name="write",
        out_shape=(
            jax.ShapeDtypeStruct((rows, inner), BF16),
            jax.ShapeDtypeStruct((inner, state), F32),
            jax.ShapeDtypeStruct((kept, 1, inner), F32),
            jax.ShapeDtypeStruct((kept, 1, 2 * state), F32),
        ),
        in_specs=[vmem()] * 5,
        out_specs=(vmem(),) * 4,
        compiler_params=pltpu.CompilerParams(vmem_limit_bytes=8 << 20),
    )(gated, scale_rows, pages, v, gain)


def crowded_pages(
    u, dt_raw, wconv_x, bconv_x, wconv_bc, bconv_bc, step_bias, decay_log, lengths, pages
):
    rows = dt_raw.shape[0]
    heads = step_bias.shape[0]
    inner = wconv_x.shape[1]
    state = wconv_bc.shape[1] // 2
    taps = wconv_x.shape[0]
    prompts = lengths.shape[0]
    nseq = lax.axis_size("seq")
    base = lax.axis_index("seq") * rows
    ends = jnp.cumsum(lengths) - 1
    starts = ends - lengths + 1
    pos = base + jnp.arange(rows, dtype=jnp.int32)
    age = pos - jnp.max(jnp.where(starts[None] <= pos[:, None], starts[None], 0), axis=1)
    weight = jnp.concatenate([wconv_x, wconv_bc], axis=1)[:, : inner + state]
    total = jnp.concatenate([bconv_x, bconv_bc])[None, : inner + state]
    joined = jnp.concatenate([u[:, :inner], u[:, 2 * inner : 2 * inner + state]], axis=1)
    for k in range(taps):
        d = taps - 1 - k
        term = joined[HALO - d : HALO - d + rows] * weight[k][None]
        total = total + jnp.where((age >= d)[:, None], term, 0.0)
    conv = jax.nn.silu(total).astype(BF16)
    x, b = conv[:, :inner], conv[:, inner:]
    dt = jax.nn.softplus(dt_raw[:, :heads] + step_bias[None])
    cum = jnp.cumsum(-dt * jnp.exp(decay_log)[None], axis=0)
    block = ends // rows
    before = jnp.concatenate([jnp.full((1,), -1, block.dtype), block[:-1]])
    after = jnp.concatenate([block[1:], jnp.full((1,), -1, block.dtype)])
    mine = (before == block) & (after == block) & (block == lax.axis_index("seq"))
    at_end = cum[jnp.clip(ends - base, 0, rows - 1)]
    keep = mine[:, None] & (pos[None] >= starts[:, None]) & (pos[None] <= ends[:, None])
    scale = jnp.where(
        keep[:, :, None], jnp.exp(jnp.minimum(at_end[:, None] - cum[None], 0.0)) * dt[None], 0.0
    )
    x_heads = x.reshape(rows, heads, -1).astype(F32)
    weighted = (scale[:, :, :, None] * x_heads[None]).astype(BF16).reshape(prompts, rows, inner)
    finals = jnp.einsum("rjc,jn->rcn", weighted, b, preferred_element_type=F32)
    hits = (pages[None, :] == jnp.arange(nseq, dtype=jnp.int32)[:, None]).astype(BF16)
    pool = jnp.einsum("qr,rcn->qcn", hits, finals.astype(BF16), preferred_element_type=F32)
    moved = lax.all_to_all(pool.astype(BF16), "seq", 0, 0, tiled=True)
    return jnp.sum(moved.astype(F32), axis=0)


def body(
    tokens, weight_x, weight_z, weight_bc, weight_dt, conv_x_weight, conv_x_bias,
    conv_bc_weight, conv_bc_bias, step_bias, decay_log, skip_gain, norm_gain, lengths, page_table,
):
    nseq, nhead = lax.axis_size("seq"), lax.axis_size("head")
    heads = weight_dt.shape[0]
    inner = weight_x.shape[1]
    width = inner // heads
    kept = conv_x_weight.shape[0] - 1
    u, dt_raw = project(tokens, weight_x, weight_z, weight_bc, weight_dt, nseq, nhead)
    gated, scale, pages, v, more = run_block(
        u, dt_raw, conv_x_weight, conv_x_bias[None, :], conv_bc_weight,
        conv_bc_bias[None, :], step_bias, decay_log, skip_gain, lengths, page_table, nseq, nhead,
    )
    normed, page, conv_x, conv_bc = write(
        gated, scale, pages, v, norm_gain[None, :], conv_bc_weight.shape[1] // 2, kept
    )
    page = lax.cond(
        more[0] > 0,
        lambda page, *rest: page + crowded_pages(*rest),
        lambda page, *rest: page,
        page, u, dt_raw, conv_x_weight, conv_x_bias, conv_bc_weight, conv_bc_bias, step_bias,
        decay_log, lengths, page_table,
    )
    return (
        normed, page.reshape(1, heads, width, -1), jnp.swapaxes(conv_x, 0, 1), jnp.swapaxes(conv_bc, 0, 1),
    )


def solution(mesh):
    in_specs = (
        P("seq", "head"), P(None, "head"), P(None, "head"), P(), P("head", None),
        P(None, "head"), P("head"), P(), P(), P("head"), P("head"), P("head"), P("head"),
        P(), P(),
    )
    out_specs = (
        P("seq", "head"), P("seq", "head", None, None), P("seq", None, "head"),
        P("seq", None, None),
    )
    return jax.shard_map(body, mesh=mesh, in_specs=in_specs, out_specs=out_specs, check_vma=False)
```

time: 78.2 us -> 60.6 us (0.77); the launches traced: 77 us -> 60.4 us
  local copies, waits for them, and re-layouts: 11.1 us -> 0.75 us
  Pallas kernels: 64.5 us -> 58.3 us
    unnamed x32 -> x22, local copies, waits for them, and re-layouts: 8.84 us -> 0.75 us
    pallas_call x2, Pallas kernels: 38.2 us -> 31.9 us  [the longest x1 30.9 us: run_block(): pl.pallas_call(functools.partial(block_kernel, xs, nseq // xs, nhead), na...]
    broadcast_in_dim x3 -> x0, local copies, waits for them, and re-layouts: 2.18 us -> none  [the longest x1 0.73 us: body(): step_bias[:, None]]
where the time goes in v2:
time: 60.6 us; the launch traced here: 60.4 us
  Pallas kernels  58.3 us (96%)
  between operations  1.37 us (2%)
  local copies, waits for them, and re-layouts  0.75 us (1%)
    pallas_call x1, Pallas kernels, run_block(): pl.pallas_call(functools.partial(block_kernel, xs, nseq // xs, nhead), na...  30.9 us
    pallas_call x1, Pallas kernels, project(): pl.pallas_call(functools.partial(project_kernel, nseq, nhead), name='proj...  26.4 us

profile of v2, /device:TPU:1, one launch (start us, length us, event | category | flops | bytes accessed | tf_op | source)
XLA Modules:
  0.0 60.4 jit_solution(215323407482418126)
XLA Ops:
  0.6 0.0 copy-start.1
  0.6 0.0 copy-start.6
  0.7 0.0 copy-start.9
  0.7 0.0 copy-start.10
  0.7 0.0 copy-start.15
  0.7 0.0 copy-start.16
  0.7 0.0 copy-start.19
  0.7 0.0 copy-start.20
  0.7 0.0 copy-start.24
  0.7 26.4 %project.1 = (f32[528,1280]{1,0:T(8,128)S(1)}, f32[512,128]{1,0:T(8,128)S(1)}) custom-call(bf16[512,256]{1,0:T(8,128)(2,1)} %tok.1, bf16[2048,512]{1,0:T(8,128)(2,1)} %wx.1, bf16[2048,512]{1,0:T(8,128)(2,1)} %wz.1, bf16[2048,256]{1,0:T(8,128)(2,1)} %wbc.1, bf16[8,2048]{1,0:T(8,128)(2,1)} %wdt.1), custom_call_target="tpu_custom_call" | custom-call | tf_op jit(solution)/shard_map/project/pallas_call | solution.py:197
  27.1 0.0 copy-done.1
  27.2 0.0 copy-done.6
  27.2 0.0 copy-done.9
  27.2 0.0 copy-done.10
  27.2 0.0 copy-done.15
  27.2 0.0 copy-done.16
  27.2 0.0 copy-done.19
  27.2 0.0 copy-done.20
  27.2 0.0 copy-done.24
  27.2 0.0 copy-start
  27.2 30.9 %block.1 = (f32[512,512]{1,0:T(8,128)S(1)}, f32[4,128]{1,0:T(4,128)S(1)}, bf16[32,16,128]{2,1,0:T(8,128)(2,1)S(1)}, f32[24,128]{1,0:T(8,128)S(1)}, s32[1]{0:T(128)}) custom-call(s32[8]{0:T(128)S(1)} %copy-done.20, s32[8]{0:T(128)S(1)} %copy-done.16, f32[8]{0:T(128)S(1)} %copy-done.19, f32[8]{0:T(128)S(1)} %copy-done.24, f32[8]{0:T(128)S(1)} %copy-done.1, ...), custom_call_target="tpu_custom_call" | custom-call | tf_op jit(solution)/shard_map/block/pallas_call | solution.py:647
  58.7 0.0 copy-done
  58.7 1.0 %write.1 = (bf16[512,512]{1,0:T(8,128)(2,1)}, f32[512,128]{1,0:T(8,128)S(1)}, f32[3,1,512]{2,1,0:T(1,128)}, f32[3,1,256]{2,1,0:T(1,128)}) custom-call(f32[512,512]{1,0:T(8,128)S(1)} %get-tuple-element.60.gated, f32[4,128]{1,0:T(4,128)S(1)} %get-tuple-element.61.scale_rows, bf16[32,16,128]{2,1,0:T(8,128)(2,1)S(1)} %get-tuple-element.62.pages, ...), custom_call_target="tpu_custom_call" | custom-call | tf_op jit(solution)/shard_map/write/pallas_call | solution.py:724
  59.7 0.0 copy-start.3
  59.7 0.7 %copy-done.3 = f32[1,8,64,128]{3,2,1,0:T(8,128)} copy-done((f32[1,8,64,128]{3,2,1,0:T(8,128)}, f32[1,8,64,128]{3,2,1,0:T(8,128)S(1)}, u32[]{:S(2)}) %copy-start.3) | copy-done | bytes 262168
  (1 shorter events, 0.0 us)
Async XLA Ops:
  0.6 26.5 %copy-start.1 = (f32[8]{0:T(128)S(1)}, f32[8]{0:T(128)}, u32[]{:S(2)}) copy-start(f32[8]{0:T(128)} %skip_gain.1) | copy-start | bytes 100
  0.6 26.5 %copy-start.6 = (f32[4,512]{1,0:T(4,128)S(1)}, f32[4,512]{1,0:T(4,128)}, u32[]{:S(2)}) copy-start(f32[4,512]{1,0:T(4,128)} %wconv_x.1) | copy-start | bytes 24580
  0.7 26.5 %copy-start.9 = (f32[4,256]{1,0:T(4,128)S(1)}, f32[4,256]{1,0:T(4,128)}, u32[]{:S(2)}) copy-start(f32[4,256]{1,0:T(4,128)} %wconv_bc.1) | copy-start | bytes 12292
  0.7 26.5 %copy-start.10 = (f32[512]{0:T(512)S(1)}, f32[512]{0:T(512)}, u32[]{:S(2)}) copy-start(f32[512]{0:T(512)} %param.23) | copy-start | bytes 6148
  0.7 26.5 %copy-start.15 = (f32[256]{0:T(256)S(1)}, f32[256]{0:T(256)}, u32[]{:S(2)}) copy-start(f32[256]{0:T(256)} %param.25) | copy-start | bytes 3076
  0.7 26.5 %copy-start.16 = (s32[8]{0:T(128)S(1)}, s32[8]{0:T(128)}, u32[]{:S(2)}) copy-start(s32[8]{0:T(128)} %page_ref.1) | copy-start | bytes 100
  0.7 26.5 %copy-start.19 = (f32[8]{0:T(128)S(1)}, f32[8]{0:T(128)}, u32[]{:S(2)}) copy-start(f32[8]{0:T(128)} %step_bias.1) | copy-start | bytes 100
  0.7 26.5 %copy-start.20 = (s32[8]{0:T(128)S(1)}, s32[8]{0:T(128)}, u32[]{:S(2)}) copy-start(s32[8]{0:T(128)} %len_ref.1) | copy-start | bytes 100
  0.7 26.5 %copy-start.24 = (f32[8]{0:T(128)S(1)}, f32[8]{0:T(128)}, u32[]{:S(2)}) copy-start(f32[8]{0:T(128)} %decay_log.1) | copy-start | bytes 100
  27.2 31.5 %copy-start = (f32[512]{0:T(512)S(1)}, f32[512]{0:T(512)}, u32[]{:S(2)}) copy-start(f32[512]{0:T(512)} %param.29) | copy-start | bytes 6148
  59.7 0.7 %copy-start.3 = (f32[1,8,64,128]{3,2,1,0:T(8,128)}, f32[1,8,64,128]{3,2,1,0:T(8,128)S(1)}, u32[]{:S(2)}) copy-start(f32[1,8,64,128]{3,2,1,0:T(8,128)S(1)} %get-tuple-element.55) | copy-start | bytes 786436

commit v3 on v2

--- a/solution.py
+++ b/solution.py
@@ -47,12 +47,12 @@
     heads = wdt.shape[0]
     yp, ym = (y + 1) % ny, (y + ny - 1) % ny
     y2 = (y + 2) % ny
-    up, down = yp * 2 + core, ym * 2 + core
     other = y * 2 + (1 - core)
     nxt, prv = (seq + 1) % nseq, (seq + nseq - 1) % nseq
     lanes = pl.ds(pl.multiple_of(core * feat, feat), feat)
     other_lanes = pl.ds(pl.multiple_of((1 - core) * feat, feat), feat)
-    first, second = pl.ds(HALO, half), pl.ds(HALO + half, half)
+    part = [pl.ds(HALO + q * half, half) for q in range(2)]
+    from_tok = [pl.ds(q * half, half) for q in range(2)]
     both = pl.ds(HALO, rows)
     edge = pl.ds(0, HALO)
 
@@ -78,35 +78,89 @@
 
     sent = []
 
-    def send(src, dst, number, to):
+    def send(src, dst, kind, q, to):
         copy = pltpu.make_async_remote_copy(
-            src_ref=src, dst_ref=dst, send_sem=ssem.at[number], recv_sem=rsem.at[number],
+            src_ref=src, dst_ref=dst, send_sem=ssem.at[kind, q], recv_sem=rsem.at[kind, q],
             device_id=to, device_id_type=MESH,
         )
         copy.start()
         sent.append(copy)
 
-    def arrive(region, number):
+    def arrive(region, kind, q):
         pltpu.make_async_remote_copy(
-            src_ref=region, dst_ref=region, send_sem=ssem.at[number], recv_sem=rsem.at[number],
+            src_ref=region, dst_ref=region, send_sem=ssem.at[kind, q], recv_sem=rsem.at[kind, q],
             device_id={"head": other}, device_id_type=MESH,
         ).wait_recv()
 
-    to_up, to_down, to_other = {"head": up}, {"head": down}, {"head": other}
+    UP, DOWN, TWO, FWD_M, FWD_P, FWD_2, OWN, EDGE = range(8)
+    to_up, to_down = {"head": yp * 2 + core}, {"head": ym * 2 + core}
+    to_other, to_two = {"head": other}, {"head": y2 * 2 + core}
+
+    def piece(owner, q, core_lanes=lanes):
+        return tokbuf.at[owner, part[q], core_lanes]
+
     mine = tokbuf.at[y]
-    send(tok.at[pl.ds(rows - HALO, HALO)], mine.at[edge, lanes], 13, {"seq": nxt})
-    send(tok.at[pl.ds(0, half)], mine.at[first, lanes], 1, to_up)
-    send(tok.at[pl.ds(half, half)], mine.at[second, lanes], 3, to_down)
-    send(tok, mine.at[both, lanes], 0, to_other)
-    send(tok.at[pl.ds(half, half)], mine.at[second, lanes], 2, to_up)
-    send(tok.at[pl.ds(0, half)], mine.at[first, lanes], 4, to_down)
+    send(tok.at[pl.ds(rows - HALO, HALO)], mine.at[edge, lanes], EDGE, 0, {"seq": nxt})
+    for q in range(2):
+        send(tok.at[from_tok[q]], piece(y, q), UP, q, to_up)
+        send(tok.at[from_tok[q]], piece(y, q), DOWN, q, to_down)
+        if q == 0:
+            send(tok, mine.at[both, lanes], OWN, 0, to_other)
+    for q in range(2):
+        send(tok.at[from_tok[q]], piece(y, q), TWO, q, to_two)
 
     def halo_piece(owner):
         return tokbuf.at[
             owner // 2, edge, pl.ds(pl.multiple_of((owner % 2) * feat, feat), feat)
         ]
 
-    arrive(halo_piece(head), 13)
+    def halo_arrive(owner):
+        pltpu.make_async_remote_copy(
+            src_ref=halo_piece(owner), dst_ref=halo_piece(owner),
+            send_sem=hs_sem.at[0], recv_sem=hr_sem.at[owner],
+            device_id={"head": other}, device_id_type=MESH,
+        ).wait_recv()
+
+    tile = 256
+    tiles = (2 * inner + wide) // tile
+
+    def multiply(at, start, low, high):
+        k = pl.ds(pl.multiple_of(at * 2 * feat, 2 * feat), 2 * feat)
+        rs = pl.ds(low, high - low)
+
+        @pl.loop(0, tiles)
+        def _(n):
+            cols = pl.ds(pl.multiple_of(n * tile, tile), tile)
+            value = jnp.dot(tokbuf[at, rs, :], w[k, cols], preferred_element_type=F32)
+            if start:
+                acc[rs, cols] = value
+            else:
+                acc[rs, cols] += value
+
+        value = lax.dot_general(
+            tokbuf[at, rs, :], wdtp[:, k], (((1,), (1,)), ((), ())),
+            preferred_element_type=F32,
+        )
+        if start:
+            accdt[rs, :] = value
+        else:
+            accdt[rs, :] += value
+
+    cut, full = HALO + half, HALO + rows
+
+    def forward(owner, q, kind, onward):
+        arrive(piece(owner, q), kind, q)
+        send(piece(owner, q), piece(owner, q), onward, q, to_other)
+
+    def halo_of(chip):
+        halo_arrive(chip * 2)
+        halo_arrive(chip * 2 + 1)
+
+    for one in loads:
+        one.wait()
+    arrive(mine.at[both, other_lanes], OWN, 0)
+    multiply(y, True, cut, full)
+    arrive(halo_piece(head), EDGE, 0)
     halo_sends = []
     for k in range(1, nhead):
         copy = pltpu.make_async_remote_copy(
@@ -117,73 +171,29 @@
         copy.start()
         halo_sends.append(copy)
 
-    def halo_arrive(owner):
-        pltpu.make_async_remote_copy(
-            src_ref=halo_piece(owner), dst_ref=halo_piece(owner),
-            send_sem=hs_sem.at[0], recv_sem=hr_sem.at[owner],
-            device_id={"head": other}, device_id_type=MESH,
-        ).wait_recv()
-
-    tile = 256
-    tiles = (2 * inner + wide) // tile
-
-    def multiply(at, start):
-        k = pl.ds(pl.multiple_of(at * 2 * feat, 2 * feat), 2 * feat)
-
-        @pl.loop(0, tiles)
-        def _(n):
-            cols = pl.ds(pl.multiple_of(n * tile, tile), tile)
-            part = jnp.dot(tokbuf[at], w[k, cols], preferred_element_type=F32)
-            if start:
-                acc[:, cols] = part
-            else:
-                acc[:, cols] += part
-
-        part = lax.dot_general(
-            tokbuf[at, both, :], wdtp[:, k], (((1,), (1,)), ((), ())),
-            preferred_element_type=F32,
-        )
-        if start:
-            accdt[...] = part
-        else:
-            accdt[...] += part
-
-    for one in loads:
-        one.wait()
-    arrive(mine.at[both, other_lanes], 0)
     halo_arrive(other)
-    multiply(y, True)
-
-    arrive(tokbuf.at[ym, first, lanes], 1)
-    send(tokbuf.at[ym, first, lanes], tokbuf.at[ym, first, lanes], 5, to_up)
-    arrive(tokbuf.at[yp, second, lanes], 3)
-    send(tokbuf.at[yp, second, lanes], tokbuf.at[yp, second, lanes], 6, to_down)
-    send(tokbuf.at[ym, first, lanes], tokbuf.at[ym, first, lanes], 7, to_other)
-    send(tokbuf.at[yp, second, lanes], tokbuf.at[yp, second, lanes], 9, to_other)
-    arrive(tokbuf.at[ym, second, lanes], 2)
-    send(tokbuf.at[ym, second, lanes], tokbuf.at[ym, second, lanes], 8, to_other)
-    arrive(tokbuf.at[yp, first, lanes], 4)
-    send(tokbuf.at[yp, first, lanes], tokbuf.at[yp, first, lanes], 10, to_other)
-    arrive(tokbuf.at[ym, first, other_lanes], 7)
-    arrive(tokbuf.at[ym, second, other_lanes], 8)
-    halo_arrive(ym * 2)
-    halo_arrive(ym * 2 + 1)
-    multiply(ym, False)
-    arrive(tokbuf.at[yp, second, other_lanes], 9)
-    arrive(tokbuf.at[yp, first, other_lanes], 10)
-    halo_arrive(yp * 2)
-    halo_arrive(yp * 2 + 1)
-    multiply(yp, False)
-
-    arrive(tokbuf.at[y2, first, lanes], 5)
-    send(tokbuf.at[y2, first, lanes], tokbuf.at[y2, first, lanes], 11, to_other)
-    arrive(tokbuf.at[y2, second, lanes], 6)
-    send(tokbuf.at[y2, second, lanes], tokbuf.at[y2, second, lanes], 12, to_other)
-    halo_arrive(y2 * 2)
-    halo_arrive(y2 * 2 + 1)
-    arrive(tokbuf.at[y2, first, other_lanes], 11)
-    arrive(tokbuf.at[y2, second, other_lanes], 12)
-    multiply(y2, False)
+    multiply(y, True, 0, cut)
+    forward(ym, 0, UP, FWD_M)
+    forward(yp, 0, DOWN, FWD_P)
+    arrive(piece(ym, 0, other_lanes), FWD_M, 0)
+    halo_of(ym)
+    multiply(ym, False, 0, cut)
+    forward(ym, 1, UP, FWD_M)
+    forward(yp, 1, DOWN, FWD_P)
+    arrive(piece(yp, 0, other_lanes), FWD_P, 0)
+    halo_of(yp)
+    multiply(yp, False, 0, cut)
+    arrive(piece(ym, 1, other_lanes), FWD_M, 1)
+    multiply(ym, False, cut, full)
+    forward(y2, 0, TWO, FWD_2)
+    arrive(piece(yp, 1, other_lanes), FWD_P, 1)
+    multiply(yp, False, cut, full)
+    forward(y2, 1, TWO, FWD_2)
+    arrive(piece(y2, 0, other_lanes), FWD_2, 0)
+    halo_of(y2)
+    multiply(y2, False, 0, cut)
+    arrive(piece(y2, 1, other_lanes), FWD_2, 1)
+    multiply(y2, False, cut, full)
 
     for copy in sent + halo_sends:
         copy.wait_send()
@@ -199,7 +209,7 @@
         name="project",
         out_shape=(
             jax.ShapeDtypeStruct((rows + HALO, total), F32),
-            jax.ShapeDtypeStruct((rows, 128), F32),
+            jax.ShapeDtypeStruct((rows + HALO, 128), F32),
         ),
         in_specs=[hbm()] * 5,
         out_specs=(vmem(), vmem()),
@@ -208,8 +218,8 @@
             pltpu.VMEM((depth, total), BF16),
             pltpu.VMEM((128, depth), BF16),
             pltpu.SemaphoreType.DMA((5,)),
-            pltpu.SemaphoreType.DMA((14,)),
-            pltpu.SemaphoreType.DMA((14,)),
+            pltpu.SemaphoreType.DMA((8, 2)),
+            pltpu.SemaphoreType.DMA((8, 2)),
             pltpu.SemaphoreType.DMA((nhead,)),
             pltpu.SemaphoreType.DMA((nhead,)),
         ],
@@ -277,7 +287,7 @@
     len_ref, page_ref, step_bias, decay_log, skip_gain,
     u, dt_raw, wconv_x, bconv_x, wconv_bc, bconv_bc,
     gated, scale_out, page_out, v_out, more_out,
-    xc, bcol, ccol, btr, scores, cols, stage, y_loc,
+    xc, bcol, btf, ccol, btr, scores, spread, cols, stage, y_loc,
     s_send, d_send, ab_send, v_all, v_send, s_buf, d_buf, ab_buf, v_buf,
     h_all, h_send, h_buf, p_send, q_send, q_buf, where_ref,
     send_sem, recv_sem, qs_sem, qr_sem,
@@ -323,7 +333,7 @@
             found = jnp.where(starts[r] <= pos, starts[r], found)
         return found
 
-    dtr = jnp.transpose(dt_raw[...])[0:heads, :]
+    dtr = jnp.transpose(dt_raw[pl.ds(HALO, rows), :])[0:heads, :]
     pre = dtr + by_head(step_bias, (heads, rows))
     dt = jnp.maximum(pre, 0.0) + jnp.log1p(jnp.exp(-jnp.abs(pre)))
     cum = -dt * jnp.exp(by_head(decay_log, (heads, rows)))
@@ -358,8 +368,7 @@
     cum2 = cum * LOG2E
     age_row = (pos - start_row).astype(F32)
     packed = jnp.concatenate(
-        [cum2, inflow, w_end, w_a, w_b, age_row]
-        + [jnp.zeros((128 - 6 * heads, rows), F32)], axis=0,
+        [cum2, inflow, age_row] + [jnp.zeros((128 - 3 * heads, rows), F32)], axis=0,
     )
     cols[...] = jnp.transpose(packed)
     low_row = lax.broadcasted_iota(jnp.int32, (1, 128), 1) < 64
@@ -378,7 +387,7 @@
     @pl.loop(0, rows // step)
     def _(t):
         r0 = pl.multiple_of(t * step, step)
-        age = jnp.broadcast_to(cols[pl.ds(r0, step), 5 * heads : 5 * heads + 1], (step, 128))
+        age = jnp.broadcast_to(cols[pl.ds(r0, step), 2 * heads : 2 * heads + 1], (step, 128))
         near = [age >= d for d in range(taps)]
         for j in range(lbs + 2):
             lanes = pl.ds(j * 128, 128)
@@ -401,19 +410,24 @@
             else:
                 ccol[pl.ds(r0, step), :] = out.astype(BF16)
 
-    btr[...] = jnp.transpose(bcol[...]).astype(BF16)
-
-    low = lax.broadcasted_iota(jnp.int32, (rows, 128), 1) < 64
-
-    def state_of(kind, lb):
-        at = (2 + kind) * heads + 2 * lb
-        scale = jnp.where(low, cols[:, at : at + 1], cols[:, at + 1 : at + 2])
-        weighted = (xc[:, pl.ds(lb * 128, 128)].astype(F32) * scale).astype(BF16)
-        value = jnp.dot(btr[...], weighted, preferred_element_type=F32)
+    btf[...] = jnp.transpose(bcol[...])
+    btr[...] = btf[...].astype(BF16)
+
+    low_state = lax.broadcasted_iota(jnp.int32, (state, 128), 1) < 64
+
+    def state_of(weight, lb):
+        pair = [
+            (btf[...] * weight[2 * lb + k : 2 * lb + k + 1, :]).astype(BF16) for k in range(2)
+        ]
+        both = jnp.dot(
+            jnp.concatenate(pair, axis=0), xc[:, pl.ds(lb * 128, 128)],
+            preferred_element_type=F32,
+        )
+        value = jnp.where(low_state, both[0:state, :], both[state:, :])
         return value.astype(BF16).reshape(per, piece, 128)
 
     for lb in range(lbs):
-        s_send[pl.ds(lb * per, per)] = state_of(0, lb)
+        s_send[pl.ds(lb * per, per)] = state_of(w_end, lb)
     pl.semaphore_wait(barrier, nseq - 1 + nhead - 1)
 
     S, D, AB, V, H, PG = range(6)
@@ -430,9 +444,10 @@
             device_id={"seq": to}, device_id_type=MESH,
         )
 
-    def out_copy(kind, n):
-        dx, dz = offset(n)
-        to = ((my_x + dx) % xs) * zs + (my_z + dz) % zs
+    x_order = [(xs // 2 + (1 - 2 * (k % 2)) * ((k + 1) // 2)) % xs for k in range(xs)]
+    x_part = [lax.rem(my_x + dx, xs) * zs for dx in x_order]
+
+    def out_copy(kind, n, to):
         if kind == S:
             return copy(S, s_send.at[to], s_buf.at[seq], n, to)
         if kind == D:
@@ -452,10 +467,17 @@
         return copy(kind, buf.at[frm], buf.at[frm], n, frm)
 
     def start_all(*kinds):
-        @pl.loop(0, nseq - 1)
-        def _(n):
+        @pl.loop(0, zs - 1)
+        def _(t):
+            dz = zs // 2 + (1 - 2 * lax.rem(t, 2)) * ((t + 1) // 2)
+            z_part = lax.rem(my_z + dz, zs)
+            for k in range(xs):
+                for kind in kinds:
+                    out_copy(kind, t * xs + k, x_part[k] + z_part).start()
+
+        for k in range(xs - 1):
             for kind in kinds:
-                out_copy(kind, n).start()
+                out_copy(kind, (zs - 1) * xs + k, x_part[k] + my_z).start()
 
     def arrive_all(*kinds):
         @pl.loop(0, nseq - 1)
@@ -465,8 +487,8 @@
 
     start_all(S, D)
     for lb in range(lbs):
-        for kind in range(2):
-            ab_send[pl.ds(lb * per, per), kind] = state_of(1 + kind, lb)
+        for kind, weight in enumerate((w_a, w_b)):
+            ab_send[pl.ds(lb * per, per), kind] = state_of(weight, lb)
     start_all(AB)
     s_buf[seq] = s_send[seq]
     d_buf[seq] = d_send[lb_me]
@@ -481,7 +503,7 @@
         gap_i = i * tile + lax.broadcasted_iota(jnp.int32, (tile, reach), 0)
         gap_j = lax.broadcasted_iota(jnp.int32, (tile, reach), 1)
         back = (gap_i - gap_j).astype(F32)
-        age = cols[ri, 5 * heads : 5 * heads + 1]
+        age = cols[ri, 2 * heads : 2 * heads + 1]
         scores[ri, 0:reach] = jnp.where((back >= 0.0) & (back <= age), sc, 0.0)
     low_t = lax.broadcasted_iota(jnp.int32, (tile, 128), 1) < 64
     for lb in range(lbs):
@@ -499,17 +521,6 @@
             y_loc[ri, lanes] = (
                 jnp.where(low_t, parts[0], parts[1]) + gain * xc[ri, lanes].astype(F32)
             )
-
-    arrive_all(S, D)
-
-    def advance(i, carried):
-        h_all[i] = carried
-        h_send[i] = carried.astype(BF16)
-        return d_buf[i, 0:1, :] * carried + s_buf[i].astype(F32)
-
-    lax.fori_loop(0, nseq, advance, jnp.zeros((piece, 128), F32))
-    start_all(H)
-    h_buf[seq] = h_send[seq]
 
     @pl.loop(0, nseq)
     def _(q):
@@ -548,6 +559,19 @@
     def _(q):
         v_send[q] = v_all[where_ref[2, q]]
 
+    arrive_all(S, D)
+
+    def advance(i, carried):
+        h_all[i] = carried
+        h_send[i] = carried.astype(BF16)
+        return d_buf[i, 0:1, :] * carried + s_buf[i].astype(F32)
+
+    lax.fori_loop(0, nseq, advance, jnp.zeros((piece, 128), F32))
+    start_all(H)
+    h_buf[seq] = h_send[seq]
+    start_all(V)
+    v_buf[seq] = v_send[seq]
+
     arrive_all(AB)
 
     @pl.loop(0, nseq)
@@ -560,15 +584,21 @@
         p_send[q] = jnp.where(kinds == 0, first, jnp.where(kinds == 1, value, 0.0)).astype(BF16)
 
     start_all(PG)
-    start_all(V)
     page_out[seq] = p_send[seq]
-    v_buf[seq] = v_send[seq]
-
-    arrive_all(H)
+
     tile = 64
     low = lax.broadcasted_iota(jnp.int32, (tile, 128), 1) < 64
     lanes128 = lax.broadcasted_iota(jnp.int32, (tile, 128), 1)
     subl = lax.broadcasted_iota(jnp.int32, (tile, 128), 0)
+    for g in range(rows // tile):
+        ri = pl.ds(g * tile, tile)
+        for lb in range(lbs):
+            lanes = pl.ds(lb * 128, 128)
+            at = heads + 2 * lb
+            scores[ri, lanes] = silu(u[pl.ds(HALO + g * tile, tile), pl.ds(inner + lb * 128, 128)])
+            spread[ri, lanes] = jnp.where(low, cols[ri, at : at + 1], cols[ri, at + 1 : at + 2])
+
+    arrive_all(H)
     for g in range(rows // 128):
         line = jnp.zeros((1, 128), F32)
         for s in range(128 // tile):
@@ -578,11 +608,8 @@
                 lanes = pl.ds(lb * 128, 128)
                 hmat = h_buf[pl.ds(lb * per, per)].reshape(state, 128)
                 ac = jnp.dot(ccol[ri, :], hmat, preferred_element_type=F32)
-                at = heads + 2 * lb
-                scale = jnp.where(low, cols[ri, at : at + 1], cols[ri, at + 1 : at + 2])
-                yv = (y_loc[ri, lanes] + ac * scale).astype(BF16).astype(F32)
-                zv = u[pl.ds(HALO + g * 128 + s * tile, tile), pl.ds(inner + lb * 128, 128)]
-                gv = yv * silu(zv)
+                yv = (y_loc[ri, lanes] + ac * spread[ri, lanes]).astype(BF16).astype(F32)
+                gv = yv * scores[ri, lanes]
                 gated[ri, lanes] = gv
                 total = total + gv * gv
             col = jnp.sum(total, axis=1, keepdims=True)
@@ -628,7 +655,7 @@
     @pl.loop(0, nseq - 1)
     def _(n):
         for kind in (S, D, AB, V, H, PG):
-            out_copy(kind, n).wait_send()
+            in_copy(kind, n).wait_send()
 
     for one in q_copies:
         one.wait_send()
@@ -636,7 +663,7 @@
 
 def run_block(u, dt_raw, wconv_x, bconv_x, wconv_bc, bconv_bc, step_bias, decay_log, skip,
               lengths, pages, nseq, nhead):
-    rows, inner = dt_raw.shape[0], wconv_x.shape[1]
+    rows, inner = dt_raw.shape[0] - HALO, wconv_x.shape[1]
     state = wconv_bc.shape[1] // 2
     lbs = inner // 128
     piece = state * lbs // nseq
@@ -659,9 +686,11 @@
         scratch_shapes=[
             pltpu.VMEM((rows, inner), BF16),
             pltpu.VMEM((rows, state), F32),
+            pltpu.VMEM((state, rows), F32),
             pltpu.VMEM((rows, state), BF16),
             pltpu.VMEM((state, rows), BF16),
-            pltpu.VMEM((rows, rows), F32),
+            pltpu.VMEM((rows, max(rows, inner)), F32),
+            pltpu.VMEM((rows, inner), F32),
             pltpu.VMEM((rows, 128), F32),
             pltpu.VMEM((v_rows, 128), F32),
             pltpu.VMEM((rows, inner), F32),
@@ -739,7 +768,7 @@
 def crowded_pages(
     u, dt_raw, wconv_x, bconv_x, wconv_bc, bconv_bc, step_bias, decay_log, lengths, pages
 ):
-    rows = dt_raw.shape[0]
+    rows = dt_raw.shape[0] - HALO
     heads = step_bias.shape[0]
     inner = wconv_x.shape[1]
     state = wconv_bc.shape[1] // 2
@@ -760,7 +789,7 @@
         total = total + jnp.where((age >= d)[:, None], term, 0.0)
     conv = jax.nn.silu(total).astype(BF16)
     x, b = conv[:, :inner], conv[:, inner:]
-    dt = jax.nn.softplus(dt_raw[:, :heads] + step_bias[None])
+    dt = jax.nn.softplus(dt_raw[HALO:, :heads] + step_bias[None])
     cum = jnp.cumsum(-dt * jnp.exp(decay_log)[None], axis=0)
     block = ends // rows
     before = jnp.concatenate([jnp.full((1,), -1, block.dtype), block[:-1]])

time: 60.6 us -> 66.8 us (1.10)
  Pallas kernels: 58.3 us -> 64.5 us
    pallas_call x1, Pallas kernels: 26.4 us -> 32.5 us  [project(): pl.pallas_call(functools.partial(project_kernel, nseq, nhead), name='proj...]
where the time goes in v3:
time: 66.8 us; the launch traced here: 66.7 us
  Pallas kernels  64.5 us (97%)
  between operations  1.44 us (2%)
  local copies, waits for them, and re-layouts  0.75 us (1%)
    pallas_call x1, Pallas kernels, project(): pl.pallas_call(functools.partial(project_kernel, nseq, nhead), name='proj...  32.5 us
    pallas_call x1, Pallas kernels, run_block(): pl.pallas_call(functools.partial(block_kernel, xs, nseq // xs, nhead), na...  31.1 us

profile of v3, /device:TPU:1, one launch (start us, length us, event | category | flops | bytes accessed | tf_op | source)
XLA Modules:
  0.0 66.7 jit_solution(8023913560851209592)
XLA Ops:
  0.6 0.0 copy-start.1
  0.6 0.0 copy-start.6
  0.7 0.0 copy-start.9
  0.7 0.0 copy-start.10
  0.7 0.0 copy-start.15
  0.7 0.0 copy-start.16
  0.7 0.0 copy-start.19
  0.7 0.0 copy-start.20
  0.7 0.0 copy-start.24
  0.7 32.5 %project.1 = (f32[528,1280]{1,0:T(8,128)S(1)}, f32[528,128]{1,0:T(8,128)S(1)}) custom-call(bf16[512,256]{1,0:T(8,128)(2,1)} %tok.1, bf16[2048,512]{1,0:T(8,128)(2,1)} %wx.1, bf16[2048,512]{1,0:T(8,128)(2,1)} %wz.1, bf16[2048,256]{1,0:T(8,128)(2,1)} %wbc.1, bf16[8,2048]{1,0:T(8,128)(2,1)} %wdt.1), custom_call_target="tpu_custom_call" | custom-call | tf_op jit(solution)/shard_map/project/pallas_call | solution.py:207
  33.2 0.0 copy-done.1
  33.2 0.0 copy-done.6
  33.2 0.0 copy-done.9
  33.3 0.0 copy-done.10
  33.3 0.0 copy-done.15
  33.3 0.0 copy-done.16
  33.3 0.0 copy-done.19
  33.3 0.0 copy-done.20
  33.3 0.0 copy-done.24
  33.3 0.0 copy-start
  33.3 31.1 %block.1 = (f32[512,512]{1,0:T(8,128)S(1)}, f32[4,128]{1,0:T(4,128)S(1)}, bf16[32,16,128]{2,1,0:T(8,128)(2,1)S(1)}, f32[24,128]{1,0:T(8,128)S(1)}, s32[1]{0:T(128)}) custom-call(s32[8]{0:T(128)S(1)} %copy-done.20, s32[8]{0:T(128)S(1)} %copy-done.16, f32[8]{0:T(128)S(1)} %copy-done.19, f32[8]{0:T(128)S(1)} %copy-done.24, f32[8]{0:T(128)S(1)} %copy-done.1, ...), custom_call_target="tpu_custom_call" | custom-call | tf_op jit(solution)/shard_map/block/pallas_call | solution.py:674
  65.0 0.0 copy-done
  65.1 1.0 %write.1 = (bf16[512,512]{1,0:T(8,128)(2,1)}, f32[512,128]{1,0:T(8,128)S(1)}, f32[3,1,512]{2,1,0:T(1,128)}, f32[3,1,256]{2,1,0:T(1,128)}) custom-call(f32[512,512]{1,0:T(8,128)S(1)} %get-tuple-element.60.gated, f32[4,128]{1,0:T(4,128)S(1)} %get-tuple-element.61.scale_rows, bf16[32,16,128]{2,1,0:T(8,128)(2,1)S(1)} %get-tuple-element.62.pages, ...), custom_call_target="tpu_custom_call" | custom-call | tf_op jit(solution)/shard_map/write/pallas_call | solution.py:753
  66.0 0.0 copy-start.3
  66.0 0.7 %copy-done.3 = f32[1,8,64,128]{3,2,1,0:T(8,128)} copy-done((f32[1,8,64,128]{3,2,1,0:T(8,128)}, f32[1,8,64,128]{3,2,1,0:T(8,128)S(1)}, u32[]{:S(2)}) %copy-start.3) | copy-done | bytes 262168
  (1 shorter events, 0.0 us)
Async XLA Ops:
  0.6 32.6 %copy-start.1 = (f32[8]{0:T(128)S(1)}, f32[8]{0:T(128)}, u32[]{:S(2)}) copy-start(f32[8]{0:T(128)} %skip_gain.1) | copy-start | bytes 100
  0.6 32.6 %copy-start.6 = (f32[4,512]{1,0:T(4,128)S(1)}, f32[4,512]{1,0:T(4,128)}, u32[]{:S(2)}) copy-start(f32[4,512]{1,0:T(4,128)} %wconv_x.1) | copy-start | bytes 24580
  0.7 32.6 %copy-start.9 = (f32[4,256]{1,0:T(4,128)S(1)}, f32[4,256]{1,0:T(4,128)}, u32[]{:S(2)}) copy-start(f32[4,256]{1,0:T(4,128)} %wconv_bc.1) | copy-start | bytes 12292
  0.7 32.6 %copy-start.10 = (f32[512]{0:T(512)S(1)}, f32[512]{0:T(512)}, u32[]{:S(2)}) copy-start(f32[512]{0:T(512)} %param.23) | copy-start | bytes 6148
  0.7 32.6 %copy-start.15 = (f32[256]{0:T(256)S(1)}, f32[256]{0:T(256)}, u32[]{:S(2)}) copy-start(f32[256]{0:T(256)} %param.25) | copy-start | bytes 3076
  0.7 32.6 %copy-start.16 = (s32[8]{0:T(128)S(1)}, s32[8]{0:T(128)}, u32[]{:S(2)}) copy-start(s32[8]{0:T(128)} %page_ref.1) | copy-start | bytes 100
  0.7 32.6 %copy-start.19 = (f32[8]{0:T(128)S(1)}, f32[8]{0:T(128)}, u32[]{:S(2)}) copy-start(f32[8]{0:T(128)} %step_bias.1) | copy-start | bytes 100
  0.7 32.6 %copy-start.20 = (s32[8]{0:T(128)S(1)}, s32[8]{0:T(128)}, u32[]{:S(2)}) copy-start(s32[8]{0:T(128)} %len_ref.1) | copy-start | bytes 100
  0.7 32.6 %copy-start.24 = (f32[8]{0:T(128)S(1)}, f32[8]{0:T(128)}, u32[]{:S(2)}) copy-start(f32[8]{0:T(128)} %decay_log.1) | copy-start | bytes 100
  33.3 31.7 %copy-start = (f32[512]{0:T(512)S(1)}, f32[512]{0:T(512)}, u32[]{:S(2)}) copy-start(f32[512]{0:T(512)} %param.29) | copy-start | bytes 6148
  66.0 0.7 %copy-start.3 = (f32[1,8,64,128]{3,2,1,0:T(8,128)}, f32[1,8,64,128]{3,2,1,0:T(8,128)S(1)}, u32[]{:S(2)}) copy-start(f32[1,8,64,128]{3,2,1,0:T(8,128)S(1)} %get-tuple-element.55) | copy-start | bytes 786436

commit v4 on v3

--- a/solution.py
+++ b/solution.py
@@ -92,9 +92,9 @@
             device_id={"head": other}, device_id_type=MESH,
         ).wait_recv()
 
-    UP, DOWN, TWO, FWD_M, FWD_P, FWD_2, OWN, EDGE = range(8)
+    UP, DOWN, RELAY, FWD_M, FWD_P, FWD_2, OWN, EDGE = range(8)
     to_up, to_down = {"head": yp * 2 + core}, {"head": ym * 2 + core}
-    to_other, to_two = {"head": other}, {"head": y2 * 2 + core}
+    to_other = {"head": other}
 
     def piece(owner, q, core_lanes=lanes):
         return tokbuf.at[owner, part[q], core_lanes]
@@ -103,12 +103,9 @@
     send(tok.at[pl.ds(rows - HALO, HALO)], mine.at[edge, lanes], EDGE, 0, {"seq": nxt})
     for q in range(2):
         send(tok.at[from_tok[q]], piece(y, q), UP, q, to_up)
-        send(tok.at[from_tok[q]], piece(y, q), DOWN, q, to_down)
+        send(tok.at[from_tok[1 - q]], piece(y, 1 - q), DOWN, 1 - q, to_down)
         if q == 0:
             send(tok, mine.at[both, lanes], OWN, 0, to_other)
-    for q in range(2):
-        send(tok.at[from_tok[q]], piece(y, q), TWO, q, to_two)
-
     def halo_piece(owner):
         return tokbuf.at[
             owner // 2, edge, pl.ds(pl.multiple_of((owner % 2) * feat, feat), feat)
@@ -171,24 +168,28 @@
         copy.start()
         halo_sends.append(copy)
 
+    arrive(piece(ym, 0), UP, 0)
+    send(piece(ym, 0), piece(ym, 0), RELAY, 0, to_up)
+    send(piece(ym, 0), piece(ym, 0), FWD_M, 0, to_other)
+    arrive(piece(yp, 1), DOWN, 1)
+    send(piece(yp, 1), piece(yp, 1), RELAY, 1, to_down)
+    send(piece(yp, 1), piece(yp, 1), FWD_P, 1, to_other)
     halo_arrive(other)
     multiply(y, True, 0, cut)
-    forward(ym, 0, UP, FWD_M)
-    forward(yp, 0, DOWN, FWD_P)
     arrive(piece(ym, 0, other_lanes), FWD_M, 0)
     halo_of(ym)
     multiply(ym, False, 0, cut)
     forward(ym, 1, UP, FWD_M)
-    forward(yp, 1, DOWN, FWD_P)
+    forward(yp, 0, DOWN, FWD_P)
+    arrive(piece(yp, 1, other_lanes), FWD_P, 1)
+    multiply(yp, False, cut, full)
+    arrive(piece(ym, 1, other_lanes), FWD_M, 1)
+    multiply(ym, False, cut, full)
+    forward(y2, 0, RELAY, FWD_2)
+    forward(y2, 1, RELAY, FWD_2)
     arrive(piece(yp, 0, other_lanes), FWD_P, 0)
     halo_of(yp)
     multiply(yp, False, 0, cut)
-    arrive(piece(ym, 1, other_lanes), FWD_M, 1)
-    multiply(ym, False, cut, full)
-    forward(y2, 0, TWO, FWD_2)
-    arrive(piece(yp, 1, other_lanes), FWD_P, 1)
-    multiply(yp, False, cut, full)
-    forward(y2, 1, TWO, FWD_2)
     arrive(piece(y2, 0, other_lanes), FWD_2, 0)
     halo_of(y2)
     multiply(y2, False, 0, cut)
@@ -640,6 +641,13 @@
         jnp.full(v_out.shape, found, jnp.int32) == 1, v_buf[source].astype(F32), 0.0
     )
 
+    arrive_all(PG)
+
+    @pl.loop(0, nseq - 1)
+    def _(n):
+        for kind in (S, D, AB, V, H, PG):
+            in_copy(kind, n).wait_send()
+
     for k in range(1, nhead):
         frm = (head + nhead - k) % nhead
         pltpu.make_async_remote_copy(
@@ -650,12 +658,6 @@
     for k in range(1, nhead):
         squares = squares + q_buf[k]
     scale_out[...] = lax.rsqrt(squares / (inner * nhead) + EPS)
-    arrive_all(PG)
-
-    @pl.loop(0, nseq - 1)
-    def _(n):
-        for kind in (S, D, AB, V, H, PG):
-            in_copy(kind, n).wait_send()
 
     for one in q_copies:
         one.wait_send()

time: 66.8 us -> 62.9 us (0.942)
  Pallas kernels: 64.5 us -> 60.6 us
    pallas_call x1, Pallas kernels: 32.5 us -> 29.2 us  [project(): pl.pallas_call(functools.partial(project_kernel, nseq, nhead), name='proj...]
where the time goes in v4:
time: 62.9 us; the launch traced here: 62.8 us
  Pallas kernels  60.6 us (96%)
  between operations  1.44 us (2%)
  local copies, waits for them, and re-layouts  0.75 us (1%)
    pallas_call x1, Pallas kernels, run_block(): pl.pallas_call(functools.partial(block_kernel, xs, nseq // xs, nhead), na...  30.4 us
    pallas_call x1, Pallas kernels, project(): pl.pallas_call(functools.partial(project_kernel, nseq, nhead), name='proj...  29.2 us

profile of v4, /device:TPU:1, one launch (start us, length us, event | category | flops | bytes accessed | tf_op | source)
XLA Modules:
  0.0 62.8 jit_solution(9909901917541847166)
XLA Ops:
  0.6 0.0 copy-start.1
  0.6 0.0 copy-start.6
  0.7 0.0 copy-start.9
  0.7 0.0 copy-start.10
  0.7 0.0 copy-start.15
  0.7 0.0 copy-start.16
  0.7 0.0 copy-start.19
  0.7 0.0 copy-start.20
  0.7 0.0 copy-start.24
  0.7 29.2 %project.1 = (f32[528,1280]{1,0:T(8,128)S(1)}, f32[528,128]{1,0:T(8,128)S(1)}) custom-call(bf16[512,256]{1,0:T(8,128)(2,1)} %tok.1, bf16[2048,512]{1,0:T(8,128)(2,1)} %wx.1, bf16[2048,512]{1,0:T(8,128)(2,1)} %wz.1, bf16[2048,256]{1,0:T(8,128)(2,1)} %wbc.1, bf16[8,2048]{1,0:T(8,128)(2,1)} %wdt.1), custom_call_target="tpu_custom_call" | custom-call | tf_op jit(solution)/shard_map/project/pallas_call | solution.py:208
  29.9 0.0 copy-done.1
  29.9 0.0 copy-done.6
  30.0 0.0 copy-done.9
  30.0 0.0 copy-done.10
  30.0 0.0 copy-done.15
  30.0 0.0 copy-done.16
  30.0 0.0 copy-done.19
  30.0 0.0 copy-done.20
  30.0 0.0 copy-done.24
  30.0 0.0 copy-start
  30.0 30.4 %block.1 = (f32[512,512]{1,0:T(8,128)S(1)}, f32[4,128]{1,0:T(4,128)S(1)}, bf16[32,16,128]{2,1,0:T(8,128)(2,1)S(1)}, f32[24,128]{1,0:T(8,128)S(1)}, s32[1]{0:T(128)}) custom-call(s32[8]{0:T(128)S(1)} %copy-done.20, s32[8]{0:T(128)S(1)} %copy-done.16, f32[8]{0:T(128)S(1)} %copy-done.19, f32[8]{0:T(128)S(1)} %copy-done.24, f32[8]{0:T(128)S(1)} %copy-done.1, ...), custom_call_target="tpu_custom_call" | custom-call | tf_op jit(solution)/shard_map/block/pallas_call | solution.py:676
  61.1 0.0 copy-done
  61.1 1.0 %write.1 = (bf16[512,512]{1,0:T(8,128)(2,1)}, f32[512,128]{1,0:T(8,128)S(1)}, f32[3,1,512]{2,1,0:T(1,128)}, f32[3,1,256]{2,1,0:T(1,128)}) custom-call(f32[512,512]{1,0:T(8,128)S(1)} %get-tuple-element.60.gated, f32[4,128]{1,0:T(4,128)S(1)} %get-tuple-element.61.scale_rows, bf16[32,16,128]{2,1,0:T(8,128)(2,1)S(1)} %get-tuple-element.62.pages, ...), custom_call_target="tpu_custom_call" | custom-call | tf_op jit(solution)/shard_map/write/pallas_call | solution.py:755
  62.1 0.0 copy-start.3
  62.1 0.7 %copy-done.3 = f32[1,8,64,128]{3,2,1,0:T(8,128)} copy-done((f32[1,8,64,128]{3,2,1,0:T(8,128)}, f32[1,8,64,128]{3,2,1,0:T(8,128)S(1)}, u32[]{:S(2)}) %copy-start.3) | copy-done | bytes 262168
  (1 shorter events, 0.0 us)
Async XLA Ops:
  0.6 29.3 %copy-start.1 = (f32[8]{0:T(128)S(1)}, f32[8]{0:T(128)}, u32[]{:S(2)}) copy-start(f32[8]{0:T(128)} %skip_gain.1) | copy-start | bytes 100
  0.6 29.3 %copy-start.6 = (f32[4,512]{1,0:T(4,128)S(1)}, f32[4,512]{1,0:T(4,128)}, u32[]{:S(2)}) copy-start(f32[4,512]{1,0:T(4,128)} %wconv_x.1) | copy-start | bytes 24580
  0.7 29.3 %copy-start.9 = (f32[4,256]{1,0:T(4,128)S(1)}, f32[4,256]{1,0:T(4,128)}, u32[]{:S(2)}) copy-start(f32[4,256]{1,0:T(4,128)} %wconv_bc.1) | copy-start | bytes 12292
  0.7 29.3 %copy-start.10 = (f32[512]{0:T(512)S(1)}, f32[512]{0:T(512)}, u32[]{:S(2)}) copy-start(f32[512]{0:T(512)} %param.23) | copy-start | bytes 6148
  0.7 29.3 %copy-start.15 = (f32[256]{0:T(256)S(1)}, f32[256]{0:T(256)}, u32[]{:S(2)}) copy-start(f32[256]{0:T(256)} %param.25) | copy-start | bytes 3076
  0.7 29.3 %copy-start.16 = (s32[8]{0:T(128)S(1)}, s32[8]{0:T(128)}, u32[]{:S(2)}) copy-start(s32[8]{0:T(128)} %page_ref.1) | copy-start | bytes 100
  0.7 29.3 %copy-start.19 = (f32[8]{0:T(128)S(1)}, f32[8]{0:T(128)}, u32[]{:S(2)}) copy-start(f32[8]{0:T(128)} %step_bias.1) | copy-start | bytes 100
  0.7 29.3 %copy-start.20 = (s32[8]{0:T(128)S(1)}, s32[8]{0:T(128)}, u32[]{:S(2)}) copy-start(s32[8]{0:T(128)} %len_ref.1) | copy-start | bytes 100
  0.7 29.3 %copy-start.24 = (f32[8]{0:T(128)S(1)}, f32[8]{0:T(128)}, u32[]{:S(2)}) copy-start(f32[8]{0:T(128)} %decay_log.1) | copy-start | bytes 100
  30.0 31.1 %copy-start = (f32[512]{0:T(512)S(1)}, f32[512]{0:T(512)}, u32[]{:S(2)}) copy-start(f32[512]{0:T(512)} %param.29) | copy-start | bytes 6148
  62.1 0.7 %copy-start.3 = (f32[1,8,64,128]{3,2,1,0:T(8,128)}, f32[1,8,64,128]{3,2,1,0:T(8,128)S(1)}, u32[]{:S(2)}) copy-start(f32[1,8,64,128]{3,2,1,0:T(8,128)S(1)} %get-tuple-element.55) | copy-start | bytes 786436

commit v5 on v2

--- a/solution.py
+++ b/solution.py
@@ -277,7 +277,7 @@
     len_ref, page_ref, step_bias, decay_log, skip_gain,
     u, dt_raw, wconv_x, bconv_x, wconv_bc, bconv_bc,
     gated, scale_out, page_out, v_out, more_out,
-    xc, bcol, ccol, btr, scores, cols, stage, y_loc,
+    xc, bcol, btf, ccol, btr, scores, spread, cols, stage, y_loc,
     s_send, d_send, ab_send, v_all, v_send, s_buf, d_buf, ab_buf, v_buf,
     h_all, h_send, h_buf, p_send, q_send, q_buf, where_ref,
     send_sem, recv_sem, qs_sem, qr_sem,
@@ -358,8 +358,7 @@
     cum2 = cum * LOG2E
     age_row = (pos - start_row).astype(F32)
     packed = jnp.concatenate(
-        [cum2, inflow, w_end, w_a, w_b, age_row]
-        + [jnp.zeros((128 - 6 * heads, rows), F32)], axis=0,
+        [cum2, inflow, age_row] + [jnp.zeros((128 - 3 * heads, rows), F32)], axis=0,
     )
     cols[...] = jnp.transpose(packed)
     low_row = lax.broadcasted_iota(jnp.int32, (1, 128), 1) < 64
@@ -378,7 +377,7 @@
     @pl.loop(0, rows // step)
     def _(t):
         r0 = pl.multiple_of(t * step, step)
-        age = jnp.broadcast_to(cols[pl.ds(r0, step), 5 * heads : 5 * heads + 1], (step, 128))
+        age = jnp.broadcast_to(cols[pl.ds(r0, step), 2 * heads : 2 * heads + 1], (step, 128))
         near = [age >= d for d in range(taps)]
         for j in range(lbs + 2):
             lanes = pl.ds(j * 128, 128)
@@ -401,19 +400,24 @@
             else:
                 ccol[pl.ds(r0, step), :] = out.astype(BF16)
 
-    btr[...] = jnp.transpose(bcol[...]).astype(BF16)
-
-    low = lax.broadcasted_iota(jnp.int32, (rows, 128), 1) < 64
-
-    def state_of(kind, lb):
-        at = (2 + kind) * heads + 2 * lb
-        scale = jnp.where(low, cols[:, at : at + 1], cols[:, at + 1 : at + 2])
-        weighted = (xc[:, pl.ds(lb * 128, 128)].astype(F32) * scale).astype(BF16)
-        value = jnp.dot(btr[...], weighted, preferred_element_type=F32)
+    btf[...] = jnp.transpose(bcol[...])
+    btr[...] = btf[...].astype(BF16)
+
+    low_state = lax.broadcasted_iota(jnp.int32, (state, 128), 1) < 64
+
+    def state_of(weight, lb):
+        pair = [
+            (btf[...] * weight[2 * lb + k : 2 * lb + k + 1, :]).astype(BF16) for k in range(2)
+        ]
+        both = jnp.dot(
+            jnp.concatenate(pair, axis=0), xc[:, pl.ds(lb * 128, 128)],
+            preferred_element_type=F32,
+        )
+        value = jnp.where(low_state, both[0:state, :], both[state:, :])
         return value.astype(BF16).reshape(per, piece, 128)
 
     for lb in range(lbs):
-        s_send[pl.ds(lb * per, per)] = state_of(0, lb)
+        s_send[pl.ds(lb * per, per)] = state_of(w_end, lb)
     pl.semaphore_wait(barrier, nseq - 1 + nhead - 1)
 
     S, D, AB, V, H, PG = range(6)
@@ -430,9 +434,10 @@
             device_id={"seq": to}, device_id_type=MESH,
         )
 
-    def out_copy(kind, n):
-        dx, dz = offset(n)
-        to = ((my_x + dx) % xs) * zs + (my_z + dz) % zs
+    x_order = [(xs // 2 + (1 - 2 * (k % 2)) * ((k + 1) // 2)) % xs for k in range(xs)]
+    x_part = [lax.rem(my_x + dx, xs) * zs for dx in x_order]
+
+    def out_copy(kind, n, to):
         if kind == S:
             return copy(S, s_send.at[to], s_buf.at[seq], n, to)
         if kind == D:
@@ -452,10 +457,17 @@
         return copy(kind, buf.at[frm], buf.at[frm], n, frm)
 
     def start_all(*kinds):
-        @pl.loop(0, nseq - 1)
-        def _(n):
+        @pl.loop(0, zs - 1)
+        def _(t):
+            dz = zs // 2 + (1 - 2 * lax.rem(t, 2)) * ((t + 1) // 2)
+            z_part = lax.rem(my_z + dz, zs)
+            for k in range(xs):
+                for kind in kinds:
+                    out_copy(kind, t * xs + k, x_part[k] + z_part).start()
+
+        for k in range(xs - 1):
             for kind in kinds:
-                out_copy(kind, n).start()
+                out_copy(kind, (zs - 1) * xs + k, x_part[k] + my_z).start()
 
     def arrive_all(*kinds):
         @pl.loop(0, nseq - 1)
@@ -465,8 +477,8 @@
 
     start_all(S, D)
     for lb in range(lbs):
-        for kind in range(2):
-            ab_send[pl.ds(lb * per, per), kind] = state_of(1 + kind, lb)
+        for kind, weight in enumerate((w_a, w_b)):
+            ab_send[pl.ds(lb * per, per), kind] = state_of(weight, lb)
     start_all(AB)
     s_buf[seq] = s_send[seq]
     d_buf[seq] = d_send[lb_me]
@@ -481,7 +493,7 @@
         gap_i = i * tile + lax.broadcasted_iota(jnp.int32, (tile, reach), 0)
         gap_j = lax.broadcasted_iota(jnp.int32, (tile, reach), 1)
         back = (gap_i - gap_j).astype(F32)
-        age = cols[ri, 5 * heads : 5 * heads + 1]
+        age = cols[ri, 2 * heads : 2 * heads + 1]
         scores[ri, 0:reach] = jnp.where((back >= 0.0) & (back <= age), sc, 0.0)
     low_t = lax.broadcasted_iota(jnp.int32, (tile, 128), 1) < 64
     for lb in range(lbs):
@@ -499,17 +511,6 @@
             y_loc[ri, lanes] = (
                 jnp.where(low_t, parts[0], parts[1]) + gain * xc[ri, lanes].astype(F32)
             )
-
-    arrive_all(S, D)
-
-    def advance(i, carried):
-        h_all[i] = carried
-        h_send[i] = carried.astype(BF16)
-        return d_buf[i, 0:1, :] * carried + s_buf[i].astype(F32)
-
-    lax.fori_loop(0, nseq, advance, jnp.zeros((piece, 128), F32))
-    start_all(H)
-    h_buf[seq] = h_send[seq]
 
     @pl.loop(0, nseq)
     def _(q):
@@ -548,6 +549,19 @@
     def _(q):
         v_send[q] = v_all[where_ref[2, q]]
 
+    arrive_all(S, D)
+
+    def advance(i, carried):
+        h_all[i] = carried
+        h_send[i] = carried.astype(BF16)
+        return d_buf[i, 0:1, :] * carried + s_buf[i].astype(F32)
+
+    lax.fori_loop(0, nseq, advance, jnp.zeros((piece, 128), F32))
+    start_all(H)
+    h_buf[seq] = h_send[seq]
+    start_all(V)
+    v_buf[seq] = v_send[seq]
+
     arrive_all(AB)
 
     @pl.loop(0, nseq)
@@ -560,15 +574,21 @@
         p_send[q] = jnp.where(kinds == 0, first, jnp.where(kinds == 1, value, 0.0)).astype(BF16)
 
     start_all(PG)
-    start_all(V)
     page_out[seq] = p_send[seq]
-    v_buf[seq] = v_send[seq]
-
-    arrive_all(H)
+
     tile = 64
     low = lax.broadcasted_iota(jnp.int32, (tile, 128), 1) < 64
     lanes128 = lax.broadcasted_iota(jnp.int32, (tile, 128), 1)
     subl = lax.broadcasted_iota(jnp.int32, (tile, 128), 0)
+    for g in range(rows // tile):
+        ri = pl.ds(g * tile, tile)
+        for lb in range(lbs):
+            lanes = pl.ds(lb * 128, 128)
+            at = heads + 2 * lb
+            scores[ri, lanes] = silu(u[pl.ds(HALO + g * tile, tile), pl.ds(inner + lb * 128, 128)])
+            spread[ri, lanes] = jnp.where(low, cols[ri, at : at + 1], cols[ri, at + 1 : at + 2])
+
+    arrive_all(H)
     for g in range(rows // 128):
         line = jnp.zeros((1, 128), F32)
         for s in range(128 // tile):
@@ -578,11 +598,8 @@
                 lanes = pl.ds(lb * 128, 128)
                 hmat = h_buf[pl.ds(lb * per, per)].reshape(state, 128)
                 ac = jnp.dot(ccol[ri, :], hmat, preferred_element_type=F32)
-                at = heads + 2 * lb
-                scale = jnp.where(low, cols[ri, at : at + 1], cols[ri, at + 1 : at + 2])
-                yv = (y_loc[ri, lanes] + ac * scale).astype(BF16).astype(F32)
-                zv = u[pl.ds(HALO + g * 128 + s * tile, tile), pl.ds(inner + lb * 128, 128)]
-                gv = yv * silu(zv)
+                yv = (y_loc[ri, lanes] + ac * spread[ri, lanes]).astype(BF16).astype(F32)
+                gv = yv * scores[ri, lanes]
                 gated[ri, lanes] = gv
                 total = total + gv * gv
             col = jnp.sum(total, axis=1, keepdims=True)
@@ -613,6 +630,13 @@
         jnp.full(v_out.shape, found, jnp.int32) == 1, v_buf[source].astype(F32), 0.0
     )
 
+    arrive_all(PG)
+
+    @pl.loop(0, nseq - 1)
+    def _(n):
+        for kind in (S, D, AB, V, H, PG):
+            in_copy(kind, n).wait_send()
+
     for k in range(1, nhead):
         frm = (head + nhead - k) % nhead
         pltpu.make_async_remote_copy(
@@ -623,12 +647,6 @@
     for k in range(1, nhead):
         squares = squares + q_buf[k]
     scale_out[...] = lax.rsqrt(squares / (inner * nhead) + EPS)
-    arrive_all(PG)
-
-    @pl.loop(0, nseq - 1)
-    def _(n):
-        for kind in (S, D, AB, V, H, PG):
-            out_copy(kind, n).wait_send()
 
     for one in q_copies:
         one.wait_send()
@@ -659,9 +677,11 @@
         scratch_shapes=[
             pltpu.VMEM((rows, inner), BF16),
             pltpu.VMEM((rows, state), F32),
+            pltpu.VMEM((state, rows), F32),
             pltpu.VMEM((rows, state), BF16),
             pltpu.VMEM((state, rows), BF16),
-            pltpu.VMEM((rows, rows), F32),
+            pltpu.VMEM((rows, max(rows, inner)), F32),
+            pltpu.VMEM((rows, inner), F32),
             pltpu.VMEM((rows, 128), F32),
             pltpu.VMEM((v_rows, 128), F32),
             pltpu.VMEM((rows, inner), F32),

time: 60.6 us -> 60.1 us (level)
  no operation moved by 1% of the time
where the time goes in v5:
time: 60.1 us; the launch traced here: 59.9 us
  Pallas kernels  57.8 us (96%)
  between operations  1.37 us (2%)
  local copies, waits for them, and re-layouts  0.75 us (1%)
    pallas_call x1, Pallas kernels, run_block(): pl.pallas_call(functools.partial(block_kernel, xs, nseq // xs, nhead), na...  30.4 us
    pallas_call x1, Pallas kernels, project(): pl.pallas_call(functools.partial(project_kernel, nseq, nhead), name='proj...  26.4 us

profile of v5, /device:TPU:1, one launch (start us, length us, event | category | flops | bytes accessed | tf_op | source)
XLA Modules:
  0.0 59.9 jit_solution(11404928878318711894)
XLA Ops:
  0.6 0.0 copy-start.1
  0.6 0.0 copy-start.6
  0.7 0.0 copy-start.9
  0.7 0.0 copy-start.10
  0.7 0.0 copy-start.15
  0.7 0.0 copy-start.16
  0.7 0.0 copy-start.19
  0.7 0.0 copy-start.20
  0.7 0.0 copy-start.24
  0.7 26.4 %project.1 = (f32[528,1280]{1,0:T(8,128)S(1)}, f32[512,128]{1,0:T(8,128)S(1)}) custom-call(bf16[512,256]{1,0:T(8,128)(2,1)} %tok.1, bf16[2048,512]{1,0:T(8,128)(2,1)} %wx.1, bf16[2048,512]{1,0:T(8,128)(2,1)} %wz.1, bf16[2048,256]{1,0:T(8,128)(2,1)} %wbc.1, bf16[8,2048]{1,0:T(8,128)(2,1)} %wdt.1), custom_call_target="tpu_custom_call" | custom-call | tf_op jit(solution)/shard_map/project/pallas_call | solution.py:197
  27.1 0.0 copy-done.1
  27.2 0.0 copy-done.6
  27.2 0.0 copy-done.9
  27.2 0.0 copy-done.10
  27.2 0.0 copy-done.15
  27.2 0.0 copy-done.16
  27.2 0.0 copy-done.19
  27.2 0.0 copy-done.20
  27.2 0.0 copy-done.24
  27.2 0.0 copy-start
  27.2 30.4 %block.1 = (f32[512,512]{1,0:T(8,128)S(1)}, f32[4,128]{1,0:T(4,128)S(1)}, bf16[32,16,128]{2,1,0:T(8,128)(2,1)S(1)}, f32[24,128]{1,0:T(8,128)S(1)}, s32[1]{0:T(128)}) custom-call(s32[8]{0:T(128)S(1)} %copy-done.20, s32[8]{0:T(128)S(1)} %copy-done.16, f32[8]{0:T(128)S(1)} %copy-done.19, f32[8]{0:T(128)S(1)} %copy-done.24, f32[8]{0:T(128)S(1)} %copy-done.1, ...), custom_call_target="tpu_custom_call" | custom-call | tf_op jit(solution)/shard_map/block/pallas_call | solution.py:665
  58.2 0.0 copy-done
  58.2 1.0 %write.1 = (bf16[512,512]{1,0:T(8,128)(2,1)}, f32[512,128]{1,0:T(8,128)S(1)}, f32[3,1,512]{2,1,0:T(1,128)}, f32[3,1,256]{2,1,0:T(1,128)}) custom-call(f32[512,512]{1,0:T(8,128)S(1)} %get-tuple-element.60.gated, f32[4,128]{1,0:T(4,128)S(1)} %get-tuple-element.61.scale_rows, bf16[32,16,128]{2,1,0:T(8,128)(2,1)S(1)} %get-tuple-element.62.pages, ...), custom_call_target="tpu_custom_call" | custom-call | tf_op jit(solution)/shard_map/write/pallas_call | solution.py:744
  59.2 0.0 copy-start.3
  59.2 0.7 %copy-done.3 = f32[1,8,64,128]{3,2,1,0:T(8,128)} copy-done((f32[1,8,64,128]{3,2,1,0:T(8,128)}, f32[1,8,64,128]{3,2,1,0:T(8,128)S(1)}, u32[]{:S(2)}) %copy-start.3) | copy-done | bytes 262168
  (1 shorter events, 0.0 us)
Async XLA Ops:
  0.6 26.5 %copy-start.1 = (f32[8]{0:T(128)S(1)}, f32[8]{0:T(128)}, u32[]{:S(2)}) copy-start(f32[8]{0:T(128)} %skip_gain.1) | copy-start | bytes 100
  0.6 26.5 %copy-start.6 = (f32[4,512]{1,0:T(4,128)S(1)}, f32[4,512]{1,0:T(4,128)}, u32[]{:S(2)}) copy-start(f32[4,512]{1,0:T(4,128)} %wconv_x.1) | copy-start | bytes 24580
  0.7 26.5 %copy-start.9 = (f32[4,256]{1,0:T(4,128)S(1)}, f32[4,256]{1,0:T(4,128)}, u32[]{:S(2)}) copy-start(f32[4,256]{1,0:T(4,128)} %wconv_bc.1) | copy-start | bytes 12292
  0.7 26.5 %copy-start.10 = (f32[512]{0:T(512)S(1)}, f32[512]{0:T(512)}, u32[]{:S(2)}) copy-start(f32[512]{0:T(512)} %param.23) | copy-start | bytes 6148
  0.7 26.5 %copy-start.15 = (f32[256]{0:T(256)S(1)}, f32[256]{0:T(256)}, u32[]{:S(2)}) copy-start(f32[256]{0:T(256)} %param.25) | copy-start | bytes 3076
  0.7 26.5 %copy-start.16 = (s32[8]{0:T(128)S(1)}, s32[8]{0:T(128)}, u32[]{:S(2)}) copy-start(s32[8]{0:T(128)} %page_ref.1) | copy-start | bytes 100
  0.7 26.5 %copy-start.19 = (f32[8]{0:T(128)S(1)}, f32[8]{0:T(128)}, u32[]{:S(2)}) copy-start(f32[8]{0:T(128)} %step_bias.1) | copy-start | bytes 100
  0.7 26.5 %copy-start.20 = (s32[8]{0:T(128)S(1)}, s32[8]{0:T(128)}, u32[]{:S(2)}) copy-start(s32[8]{0:T(128)} %len_ref.1) | copy-start | bytes 100
  0.7 26.5 %copy-start.24 = (f32[8]{0:T(128)S(1)}, f32[8]{0:T(128)}, u32[]{:S(2)}) copy-start(f32[8]{0:T(128)} %decay_log.1) | copy-start | bytes 100
  27.2 31.0 %copy-start = (f32[512]{0:T(512)S(1)}, f32[512]{0:T(512)}, u32[]{:S(2)}) copy-start(f32[512]{0:T(512)} %param.29) | copy-start | bytes 6148
  59.2 0.7 %copy-start.3 = (f32[1,8,64,128]{3,2,1,0:T(8,128)}, f32[1,8,64,128]{3,2,1,0:T(8,128)S(1)}, u32[]{:S(2)}) copy-start(f32[1,8,64,128]{3,2,1,0:T(8,128)S(1)} %get-tuple-element.55) | copy-start | bytes 786436

commit v6 on v5

--- a/solution.py
+++ b/solution.py
@@ -152,12 +152,12 @@
         one.wait()
     arrive(mine.at[both, other_lanes], 0)
     halo_arrive(other)
-    multiply(y, True)
-
     arrive(tokbuf.at[ym, first, lanes], 1)
     send(tokbuf.at[ym, first, lanes], tokbuf.at[ym, first, lanes], 5, to_up)
     arrive(tokbuf.at[yp, second, lanes], 3)
     send(tokbuf.at[yp, second, lanes], tokbuf.at[yp, second, lanes], 6, to_down)
+    multiply(y, True)
+
     send(tokbuf.at[ym, first, lanes], tokbuf.at[ym, first, lanes], 7, to_other)
     send(tokbuf.at[yp, second, lanes], tokbuf.at[yp, second, lanes], 9, to_other)
     arrive(tokbuf.at[ym, second, lanes], 2)

time: 60.1 us -> 61.1 us (1.017); the launches traced: 59.9 us -> 59.9 us
    pallas_call x1, Pallas kernels: 30.4 us -> 29.3 us  [run_block(): pl.pallas_call(functools.partial(block_kernel, xs, nseq // xs, nhead), na...]
    pallas_call x1, Pallas kernels: 26.4 us -> 27.5 us  [project(): pl.pallas_call(functools.partial(project_kernel, nseq, nhead), name='proj...]
where the time goes in v6:
time: 61.1 us; the launch traced here: 59.9 us
  Pallas kernels  57.8 us (95%)
  between operations  1.37 us (2%)
  local copies, waits for them, and re-layouts  0.75 us (1%)
    pallas_call x1, Pallas kernels, run_block(): pl.pallas_call(functools.partial(block_kernel, xs, nseq // xs, nhead), na...  29.3 us
    pallas_call x1, Pallas kernels, project(): pl.pallas_call(functools.partial(project_kernel, nseq, nhead), name='proj...  27.5 us

profile of v6, /device:TPU:1, one launch (start us, length us, event | category | flops | bytes accessed | tf_op | source)
XLA Modules:
  0.0 59.9 jit_solution(2913308235211546376)
XLA Ops:
  0.6 0.0 copy-start.1
  0.6 0.0 copy-start.6
  0.7 0.0 copy-start.9
  0.7 0.0 copy-start.10
  0.7 0.0 copy-start.15
  0.7 0.0 copy-start.16
  0.7 0.0 copy-start.19
  0.7 0.0 copy-start.20
  0.7 0.0 copy-start.24
  0.7 27.5 %project.1 = (f32[528,1280]{1,0:T(8,128)S(1)}, f32[512,128]{1,0:T(8,128)S(1)}) custom-call(bf16[512,256]{1,0:T(8,128)(2,1)} %tok.1, bf16[2048,512]{1,0:T(8,128)(2,1)} %wx.1, bf16[2048,512]{1,0:T(8,128)(2,1)} %wz.1, bf16[2048,256]{1,0:T(8,128)(2,1)} %wbc.1, bf16[8,2048]{1,0:T(8,128)(2,1)} %wdt.1), custom_call_target="tpu_custom_call" | custom-call | tf_op jit(solution)/shard_map/project/pallas_call | solution.py:197
  28.2 0.0 copy-done.1
  28.2 0.0 copy-done.6
  28.2 0.0 copy-done.9
  28.2 0.0 copy-done.10
  28.2 0.0 copy-done.15
  28.3 0.0 copy-done.16
  28.3 0.0 copy-done.19
  28.3 0.0 copy-done.20
  28.3 0.0 copy-done.24
  28.3 0.0 copy-start
  28.3 29.3 %block.1 = (f32[512,512]{1,0:T(8,128)S(1)}, f32[4,128]{1,0:T(4,128)S(1)}, bf16[32,16,128]{2,1,0:T(8,128)(2,1)S(1)}, f32[24,128]{1,0:T(8,128)S(1)}, s32[1]{0:T(128)}) custom-call(s32[8]{0:T(128)S(1)} %copy-done.20, s32[8]{0:T(128)S(1)} %copy-done.16, f32[8]{0:T(128)S(1)} %copy-done.19, f32[8]{0:T(128)S(1)} %copy-done.24, f32[8]{0:T(128)S(1)} %copy-done.1, ...), custom_call_target="tpu_custom_call" | custom-call | tf_op jit(solution)/shard_map/block/pallas_call | solution.py:665
  58.2 0.0 copy-done
  58.2 1.0 %write.1 = (bf16[512,512]{1,0:T(8,128)(2,1)}, f32[512,128]{1,0:T(8,128)S(1)}, f32[3,1,512]{2,1,0:T(1,128)}, f32[3,1,256]{2,1,0:T(1,128)}) custom-call(f32[512,512]{1,0:T(8,128)S(1)} %get-tuple-element.60.gated, f32[4,128]{1,0:T(4,128)S(1)} %get-tuple-element.61.scale_rows, bf16[32,16,128]{2,1,0:T(8,128)(2,1)S(1)} %get-tuple-element.62.pages, ...), custom_call_target="tpu_custom_call" | custom-call | tf_op jit(solution)/shard_map/write/pallas_call | solution.py:744
  59.2 0.0 copy-start.3
  59.2 0.7 %copy-done.3 = f32[1,8,64,128]{3,2,1,0:T(8,128)} copy-done((f32[1,8,64,128]{3,2,1,0:T(8,128)}, f32[1,8,64,128]{3,2,1,0:T(8,128)S(1)}, u32[]{:S(2)}) %copy-start.3) | copy-done | bytes 262168
  (1 shorter events, 0.0 us)
Async XLA Ops:
  0.6 27.6 %copy-start.1 = (f32[8]{0:T(128)S(1)}, f32[8]{0:T(128)}, u32[]{:S(2)}) copy-start(f32[8]{0:T(128)} %skip_gain.1) | copy-start | bytes 100
  0.6 27.6 %copy-start.6 = (f32[4,512]{1,0:T(4,128)S(1)}, f32[4,512]{1,0:T(4,128)}, u32[]{:S(2)}) copy-start(f32[4,512]{1,0:T(4,128)} %wconv_x.1) | copy-start | bytes 24580
  0.7 27.6 %copy-start.9 = (f32[4,256]{1,0:T(4,128)S(1)}, f32[4,256]{1,0:T(4,128)}, u32[]{:S(2)}) copy-start(f32[4,256]{1,0:T(4,128)} %wconv_bc.1) | copy-start | bytes 12292
  0.7 27.6 %copy-start.10 = (f32[512]{0:T(512)S(1)}, f32[512]{0:T(512)}, u32[]{:S(2)}) copy-start(f32[512]{0:T(512)} %param.23) | copy-start | bytes 6148
  0.7 27.6 %copy-start.15 = (f32[256]{0:T(256)S(1)}, f32[256]{0:T(256)}, u32[]{:S(2)}) copy-start(f32[256]{0:T(256)} %param.25) | copy-start | bytes 3076
  0.7 27.6 %copy-start.16 = (s32[8]{0:T(128)S(1)}, s32[8]{0:T(128)}, u32[]{:S(2)}) copy-start(s32[8]{0:T(128)} %page_ref.1) | copy-start | bytes 100
  0.7 27.6 %copy-start.19 = (f32[8]{0:T(128)S(1)}, f32[8]{0:T(128)}, u32[]{:S(2)}) copy-start(f32[8]{0:T(128)} %step_bias.1) | copy-start | bytes 100
  0.7 27.6 %copy-start.20 = (s32[8]{0:T(128)S(1)}, s32[8]{0:T(128)}, u32[]{:S(2)}) copy-start(s32[8]{0:T(128)} %len_ref.1) | copy-start | bytes 100
  0.7 27.6 %copy-start.24 = (f32[8]{0:T(128)S(1)}, f32[8]{0:T(128)}, u32[]{:S(2)}) copy-start(f32[8]{0:T(128)} %decay_log.1) | copy-start | bytes 100
  28.3 29.9 %copy-start = (f32[512]{0:T(512)S(1)}, f32[512]{0:T(512)}, u32[]{:S(2)}) copy-start(f32[512]{0:T(512)} %param.29) | copy-start | bytes 6148
  59.2 0.7 %copy-start.3 = (f32[1,8,64,128]{3,2,1,0:T(8,128)}, f32[1,8,64,128]{3,2,1,0:T(8,128)S(1)}, u32[]{:S(2)}) copy-start(f32[1,8,64,128]{3,2,1,0:T(8,128)S(1)} %get-tuple-element.55) | copy-start | bytes 786436
